TPU v7x, 32 devices: a whole 2x2x4 slice. The times are simulated.
32 devices in a mesh: grp: 8 (over y, x, core), blk: 4 (over z).
Axes of the slice: x: 2, y: 2, z: 4, core: 2. Of those that a mesh axis runs over, the one named last changes fastest.
Arguments:
- embed: bfloat16 [16384, 1024], P(('grp', 'blk')), may hold values from -6 to 6
- dest: int32 [16384], P(('grp', 'blk')), may hold values from 0 to 31, as said below
- slot: int32 [16384], P(('grp', 'blk')), may hold values from 0 to 511, as said below
Outputs:
- best: float32 [16384], P(('grp', 'blk'))
Inputs may be any that keep to these rules, and one draw needn't show every extreme that they name: Each device index receives exactly 512 documents; at most 32 documents of one device's rows name the same dest, and in every draw some device sends exactly 32 to some dest. The pairs (dest, slot) are all different.
All inputs are finite; a program needn't handle non-finite values.
Results may differ from a plain program's by a relative error of at most 0.0013.
Values may be sent and summed in bfloat16 or wider, within the bound.
No kernel may reach another device: no remote copies, remote signals or barrier semaphores. Data moves between devices by JAX's collectives and lax.ppermute only.
A program may use at most 64 MiB of HBM per device.

v0:
```python
import functools

import jax
import jax.numpy as jnp
from jax import lax
from jax.experimental import pallas as pl
from jax.experimental.pallas import tpu as pltpu
from jax.sharding import PartitionSpec as P


AXES = ("grp", "blk")
PAD = 2.0
LOW = -8.0
FULL = 4.0
REDO = 100.0
F32 = jnp.float32
BF16 = jnp.bfloat16
VMEM = pl.BlockSpec(memory_space=pltpu.VMEM)
SMEM = pl.BlockSpec(memory_space=pltpu.SMEM)
TILE = 256


def pack_kernel(nsec, cap, nblk, me_ref, dest_ref, embed_ref, *outs):
    pos_ref, sections = outs[0], outs[1:]
    count = embed_ref.shape[0]
    cluster = lax.div(dest_ref[...], nblk)
    part = cluster ^ me_ref[0]
    onehot = lax.broadcasted_iota(jnp.int32, (nsec, count), 0) == part
    lower = lax.broadcasted_iota(jnp.int32, (count, count), 0) < lax.broadcasted_iota(
        jnp.int32, (count, count), 1
    )
    before = jnp.dot(
        onehot.astype(F32).astype(BF16), lower.astype(F32).astype(BF16), preferred_element_type=F32
    )
    rank = jnp.sum(jnp.where(onehot, before, 0.0), axis=0, keepdims=True).astype(jnp.int32)
    pos = part * cap + rank
    pos_ref[...] = cluster * cap + rank
    wide = embed_ref[...].astype(F32)
    unit = (wide * lax.rsqrt(jnp.sum(wide * wide, axis=1, keepdims=True) + 1e-06)).astype(BF16)
    held = jnp.sum(onehot.astype(F32), axis=1, keepdims=True)
    rows = lax.broadcasted_iota(jnp.int32, (cap, 128), 0).astype(F32)
    first = lax.broadcasted_iota(jnp.int32, (cap, 128), 1) == 0
    for k, out in enumerate(sections):
        pick = lax.broadcasted_iota(jnp.int32, (cap, count), 0) + k * cap == pos
        out[...] = jnp.dot(
            pick.astype(F32).astype(BF16), unit, preferred_element_type=F32
        ).astype(BF16)
        mark = jnp.where(first & (rows >= held[k : k + 1, :]), PAD, 0.0)
        out[:, 0:128] = (out[:, 0:128].astype(F32) + mark).astype(BF16)


def pack(embed, dest, me, nsec, cap, nblk):
    count, width = embed.shape
    return pl.pallas_call(
        functools.partial(pack_kernel, nsec, cap, nblk),
        out_shape=[jax.ShapeDtypeStruct((1, count), jnp.int32)]
        + [jax.ShapeDtypeStruct((cap, width), BF16)] * nsec,
        in_specs=[SMEM, VMEM, VMEM],
        out_specs=[VMEM] * (nsec + 1),
        compiler_params=pltpu.CompilerParams(vmem_limit_bytes=24 << 20),
        name="pack",
    )(me, dest.reshape(1, count), embed)


def scores(left, right):
    return lax.dot_general(left, right, (((1,), (1,)), ((), ())), preferred_element_type=F32)


def first_entries(rows_ref):
    first = lax.broadcasted_iota(jnp.int32, (8, rows_ref.shape[1]), 1) == 0
    return scores(first.astype(F32).astype(BF16), rows_ref[...])[0:1, :]


def squeeze_kernel(nsec, *refs):
    sections, out_ref, pos_ref = refs[:nsec], refs[nsec], refs[nsec + 1]
    room = out_ref.shape[0]
    cap = sections[0].shape[0]
    size = nsec * cap
    filled = jnp.concatenate([first_entries(s) for s in sections], axis=1) < 1.5
    lower = lax.broadcasted_iota(jnp.int32, (size, size), 0) < lax.broadcasted_iota(
        jnp.int32, (size, size), 1
    )
    ones = jnp.broadcast_to(filled.astype(F32), (8, size))
    before = jnp.dot(
        ones.astype(BF16), lower.astype(F32).astype(BF16), preferred_element_type=F32
    )[0:1, :]
    total = jnp.sum(filled.astype(F32), axis=1, keepdims=True)
    pos = jnp.where(filled, before, -1.0).astype(jnp.int32)
    pos_ref[...] = pos
    pick = (lax.broadcasted_iota(jnp.int32, (room, size), 0) == pos).astype(F32).astype(BF16)
    value = jnp.dot(pick[:, 0:cap], sections[0][...], preferred_element_type=F32)
    for k in range(1, nsec):
        value = value + jnp.dot(
            pick[:, k * cap : (k + 1) * cap], sections[k][...], preferred_element_type=F32
        )
    out_ref[...] = value.astype(BF16)
    rows = lax.broadcasted_iota(jnp.int32, (room, 128), 0).astype(F32)
    first = lax.broadcasted_iota(jnp.int32, (room, 128), 1) == 0
    head = jnp.where(first & (rows >= total), PAD, value[:, 0:128])
    head = jnp.where(first & (rows == room - 1.0) & (total > room), FULL, head)
    out_ref[:, 0:128] = head.astype(BF16)


def squeeze(sections, room):
    cap, width = sections[0].shape
    size = len(sections) * cap
    return pl.pallas_call(
        functools.partial(squeeze_kernel, len(sections)),
        out_shape=[
            jax.ShapeDtypeStruct((room, width), BF16),
            jax.ShapeDtypeStruct((1, size), jnp.int32),
        ],
        in_specs=[VMEM] * len(sections),
        out_specs=[VMEM] * 2,
        compiler_params=pltpu.CompilerParams(vmem_limit_bytes=12 << 20),
        cost_estimate=pl.CostEstimate(
            flops=2 * room * size * width, bytes_accessed=2 * (room + size) * width, transcendentals=0
        ),
        name="squeeze",
    )(*sections)


def bias_of(entries):
    return jnp.where(entries > 3.0, REDO, jnp.where(entries > 1.5, LOW, 0.0))


def pair_kernel(nblk, nold, unroll, owner_ref, *refs):
    refs = list(refs)
    take = lambda n: [refs.pop(0) for _ in range(n)]
    blocks, olds, bias_olds, best_olds = take(nblk), take(nold), take(nold), take(nold)
    (new_ref, bias_ref, best_ref), best_outs = take(3), take(nold)
    (acc_ref,) = take(1)
    rows, size = new_ref.shape[0], blocks[0].shape[0]
    tiles = lambda n: [(lo, min(TILE, n - lo)) for lo in range(0, n, TILE)]

    @pl.when(owner_ref[0] == 1)
    def _():
        for j, block in enumerate(blocks):
            new_ref[j * size : (j + 1) * size, :] = block[...]
        bias_ref[...] = bias_of(first_entries(new_ref))
        down = bias_of(new_ref[:, 0:1].astype(F32))
        acc_ref[...] = jnp.full_like(acc_ref, LOW)

        def fold(start, value):
            part = value[:, 0:128]
            for j in range(1, value.shape[1] // 128):
                part = jnp.maximum(part, value[:, j * 128 : (j + 1) * 128])
            acc_ref[start:, :] = jnp.maximum(acc_ref[start:, :], part)

        col_best = []
        for lo, tile in tiles(rows):
            value = scores(new_ref[lo:, :], new_ref[lo : lo + tile, :])
            same = lax.broadcasted_iota(jnp.int32, value.shape, 0) == lax.broadcasted_iota(
                jnp.int32, value.shape, 1
            )
            value = jnp.where(same, LOW, value)
            fold(lo, value + bias_ref[:, lo : lo + tile])
            col_best.append(jnp.max(value + down[lo:, :], axis=0, keepdims=True))
        for old, bias, best, out in zip(olds, bias_olds, best_olds, best_outs):

            def step(i, carry, old=old, bias=bias, best=best, out=out, tile=TILE):
                at = pl.ds(i * TILE, tile) if tile < TILE else pl.ds(pl.multiple_of(i * TILE, TILE), TILE)
                value = scores(new_ref[...], old[at, :])
                fold(0, value + bias[:, at])
                out[:, at] = jnp.maximum(
                    best[:, at], jnp.max(value + down, axis=0, keepdims=True)
                )
                return carry

            full, rest = divmod(old.shape[0], TILE)
            lax.fori_loop(0, full, step, 0, unroll=unroll if full % unroll == 0 else full)
            if rest:
                step(full, 0, tile=rest)
        for j, (lo, tile) in enumerate(tiles(rows)):
            across = jnp.max(acc_ref[lo : lo + tile, :].T, axis=0, keepdims=True)
            best_ref[:, lo : lo + tile] = jnp.maximum(across, col_best[j])


def ceil_to(n, m):
    return -(-n // m) * m


def pair(owner, blocks, olds, biases, bests, unroll):
    nblk, (size, width) = len(blocks), blocks[0].shape
    rows, nold = nblk * size, len(olds)
    row = jax.ShapeDtypeStruct((1, rows), F32)
    flops = 2 * width * rows * (rows // 2 + sum(o.shape[0] for o in olds))
    out = pl.pallas_call(
        functools.partial(pair_kernel, nblk, nold, unroll),
        out_shape=[jax.ShapeDtypeStruct((rows, width), BF16), row, row]
        + [jax.ShapeDtypeStruct(b.shape, F32) for b in bests],
        in_specs=[SMEM] + [VMEM] * (nblk + 3 * nold),
        out_specs=[VMEM] * (3 + nold),
        scratch_shapes=[pltpu.VMEM((rows, 128), F32)],
        compiler_params=pltpu.CompilerParams(vmem_limit_bytes=24 << 20),
        cost_estimate=pl.CostEstimate(
            flops=flops, bytes_accessed=rows * width * 2, transcendentals=0
        ),
        name="pair",
    )(owner, *blocks, *olds, *biases, *bests)
    return out[0], out[1], list(out[3:]) + [out[2]]


def every_kernel(nblk, owner_ref, *refs):
    blocks, best_ref, all_ref = refs[:nblk], refs[nblk], refs[nblk + 1]
    size = blocks[0].shape[0]
    count = nblk * size // TILE

    @pl.when(owner_ref[0] == 1)
    def _():
        for j, block in enumerate(blocks):
            all_ref[j * size : (j + 1) * size, :] = block[...]
        same = lax.broadcasted_iota(jnp.int32, (TILE, TILE), 0) == lax.broadcasted_iota(
            jnp.int32, (TILE, TILE), 1
        )
        span = lambda i: pl.ds(pl.multiple_of(i * TILE, TILE), TILE)

        def column(j, carry):
            def row(i, best):
                rows = all_ref[span(i), :]
                value = scores(rows, all_ref[span(j), :]) + bias_of(rows[:, 0:1].astype(F32))
                value = jnp.where(same & (i == j), LOW, value)
                return jnp.maximum(best, jnp.max(value, axis=0, keepdims=True))

            best_ref[:, span(j)] = lax.fori_loop(0, count, row, jnp.full((1, TILE), LOW, F32))
            return carry

        lax.fori_loop(0, count, column, 0)


def every(owner, blocks):
    nblk, (size, width) = len(blocks), blocks[0].shape
    return pl.pallas_call(
        functools.partial(every_kernel, nblk),
        out_shape=jax.ShapeDtypeStruct((1, nblk * size), F32),
        in_specs=[SMEM] + [VMEM] * nblk,
        out_specs=VMEM,
        scratch_shapes=[pltpu.VMEM((nblk * size, width), BF16)],
        compiler_params=pltpu.CompilerParams(vmem_limit_bytes=28 << 20),
        name="every",
    )(owner, *blocks)


def spread_kernel(nq, nblk, counts, zs, owner_ref, me_ref, *refs):
    bests, places, out_ref, rows_ref = refs[:nq], refs[nq : nq + nblk], refs[-2], refs[-1]
    cap = out_ref.shape[2]

    @pl.when(owner_ref[0] == 1)
    def _():
        me = me_ref[0]
        top = functools.reduce(jnp.maximum, [jnp.max(b[...]) for b in bests])
        k = 0
        for best, ns in zip(bests, counts):
            size = best.shape[1] // nblk
            for j in range(nblk):
                rows_ref[j : j + 1, 0:size] = best[:, j * size : (j + 1) * size]
            turned = rows_ref[...].T
            lo = k * cap
            for j, zz in enumerate(zs):
                pos = places[j][:, lo : lo + ns * cap]
                hit = lax.broadcasted_iota(jnp.int32, (size, ns * cap), 0) == pos
                back = jnp.max(
                    jnp.where(hit, turned[0:size, j : j + 1], LOW), axis=0, keepdims=True
                )
                back = jnp.where(pos < 0, top, back)
                z = jnp.where(me % 2 == 0, zz, nblk - 1 - zz)
                for i in range(ns):
                    out_ref[((k + i) ^ me) * nblk + z] = back[:, i * cap : (i + 1) * cap]
            k += ns


def spread(owner, me, bests, places, counts, zs, nsec, cap):
    nblk = len(zs)
    widest = max(b.shape[1] for b in bests) // nblk
    return pl.pallas_call(
        functools.partial(spread_kernel, len(bests), nblk, counts, zs),
        out_shape=jax.ShapeDtypeStruct((nsec * nblk, 1, cap), F32),
        in_specs=[SMEM, SMEM] + [VMEM] * (len(bests) + nblk),
        out_specs=VMEM,
        scratch_shapes=[pltpu.VMEM((ceil_to(nblk, 8), ceil_to(widest, 128)), F32)],
        compiler_params=pltpu.CompilerParams(vmem_limit_bytes=8 << 20),
        name="spread",
    )(owner, me, *bests, *places)


def pick_kernel(nsec, nblk, pos_ref, got_ref, out_ref, redo_ref):
    count, cap = pos_ref.shape[1], got_ref.shape[2]
    got = jnp.concatenate([got_ref[c * nblk + nblk // 2 - c % 2] for c in range(nsec)], axis=0)
    redo_ref[0] = (jnp.max(got) > 0.5 * REDO).astype(jnp.int32)
    turned = got.T
    total = jnp.zeros((1, count), F32)
    for c in range(nsec):
        hit = lax.broadcasted_iota(jnp.int32, (cap, count), 0) + c * cap == pos_ref[...]
        total = total + jnp.sum(jnp.where(hit, turned[:, c : c + 1], 0.0), axis=0, keepdims=True)
    out_ref[...] = total


def pick(pos, got, nsec, nblk):
    return pl.pallas_call(
        functools.partial(pick_kernel, nsec, nblk),
        out_shape=[
            jax.ShapeDtypeStruct(pos.shape, F32),
            jax.ShapeDtypeStruct((1,), jnp.int32),
        ],
        in_specs=[VMEM, VMEM],
        out_specs=[VMEM, SMEM],
        compiler_params=pltpu.CompilerParams(vmem_limit_bytes=8 << 20),
        name="pick",
    )(pos, got)


def xor(nsec, bits):
    return [(g, g ^ bits) for g in range(nsec)]


def best_of_all(held, owner, me, pos, parts, share, nblk):
    nsec, cap = len(held), held[0].shape[0]
    upper = nblk // 2
    order = sorted((z for z in range(nblk) if z != upper), key=lambda z: abs(z - upper))
    flip = lambda b, core: b if core == 0 else nblk - 1 - b
    routes = [
        [(g * nblk + flip(z, g % 2), g * nblk + flip(upper, g % 2)) for g in range(nsec)]
        for z in order
    ]
    arrays, biases, bests, places = [], [], [], []
    for q, (lo, hi) in enumerate(parts):
        group, place = squeeze(held[lo:hi], share[q] * (hi - lo) * cap // 16)
        places.append(place)
        blocks = [group]
        for route in routes:
            blocks.append(lax.ppermute(group, AXES, route))
        if len(parts) == 1:
            bests = [every(owner, blocks)]
        else:
            new, bias, bests = pair(owner, blocks, arrays, biases, bests, 3)
            arrays.append(new)
            biases.append(bias)
    place = jnp.concatenate(places, axis=1)
    spots = [place]
    for route in routes:
        spots.append(lax.ppermute(place, AXES, route))
    counts = tuple(hi - lo for lo, hi in parts)
    sorted_out = spread(owner, me, bests, spots, counts, (upper, *order), nsec, cap)
    got = lax.all_to_all(sorted_out, AXES, split_axis=0, concat_axis=0, tiled=True)
    return pick(pos, got, nsec, nblk)


def on_device(embed, dest, slot):
    count = embed.shape[0]
    nsec, nblk = lax.axis_size("grp"), lax.axis_size("blk")
    cap = 2 * count // (nsec * nblk) * nblk
    grp, blk = lax.axis_index("grp"), lax.axis_index("blk")
    me = grp.astype(jnp.int32).reshape(1)
    owner = (blk == nblk // 2 - grp % 2).astype(jnp.int32).reshape(1)
    pos, *sent = pack(embed, dest, me, nsec, cap, nblk)
    quarter = nsec // 4
    parts = [(0, quarter), (quarter, 3 * quarter), (3 * quarter, nsec)]
    held = [sent[0]]
    for k in range(1, nsec):
        held.append(lax.ppermute(sent[k], "grp", xor(nsec, k)))
    best, redo = best_of_all(held, owner, me, pos, parts, (12, 11, 12), nblk)
    best = lax.cond(
        redo[0] > 0,
        lambda: best_of_all(held, owner, me, pos, [(0, nsec)], (16,), nblk)[0],
        lambda: best,
    )
    return best.reshape(count)


def solution(mesh):
    placed = (P(AXES, None), P(AXES), P(AXES))
    return jax.shard_map(
        on_device, mesh=mesh, in_specs=placed, out_specs=P(AXES), check_vma=False
    )
```

profile of v0, /device:TPU:0, one launch (start us, length us, event | category | flops | bytes accessed | tf_op | source)
XLA Modules:
  0.0 101.9 jit_solution(8236528598508980879)
XLA Ops:
  0.0 1.2 %copy-done = bf16[512,1024]{1,0:T(8,128)(2,1)S(1)} copy-done((bf16[512,1024]{1,0:T(8,128)(2,1)S(1)}, bf16[512,1024]{1,0:T(8,128)(2,1)}, u32[]{:S(2)}) %copy-start) | copy-done | bytes 1048600
  1.2 0.7 copy-done.1
  1.9 1.7 %pack.1 = (s32[1,512]{1,0:T(1,128)S(1)}, bf16[128,1024]{1,0:T(8,128)(2,1)S(1)}, bf16[128,1024]{1,0:T(8,128)(2,1)S(1)}, bf16[128,1024]{1,0:T(8,128)(2,1)S(1)}, bf...) custom-call(s32[1]{0:T(128)} %bitcast.2.me_ref, ...), custom_call_target="tpu_custom_call" | custom-call | tf_op jit(solution)/shard_map/pack/pallas_call | solution.py:54
  3.6 0.6 collective-permute-start.11
  4.2 2.5 %collective-permute-start.15 = (bf16[128,1024]{1,0:T(8,128)(2,1)S(1)}, bf16[128,1024]{1,0:T(8,128)(2,1)S(1)}, u32[]{:S(2)}, u32[]{:S(2)}) collective-permute-start(bf16[128,1024]{1,0:T(8,128)(2,1)S(1)} %get-tuple-element.82), channel_id=1, source_target_pairs={{0,8},{4,12},{8,0},{12,4},{16,24},{20,28},{24,16},{28,20},{1,9},{5... | collective-permute-start | bytes 786440 | tf_op jit(solution)/shard_map/ppermute | solution.py:360
  6.7 0.0 collective-permute-start.16
  6.8 1.8 %collective-permute-start.17 = (bf16[128,1024]{1,0:T(8,128)(2,1)S(1)}, bf16[128,1024]{1,0:T(8,128)(2,1)S(1)}, u32[]{:S(2)}, u32[]{:S(2)}) collective-permute-start(bf16[128,1024]{1,0:T(8,128)(2,1)S(1)} %get-tuple-element.84), channel_id=1, source_target_pairs={{0,16},{4,20},{8,24},{12,28},{16,0},{20,4},{24,8},{28,12},{1,17},{... | collective-permute-start | bytes 786440 | tf_op jit(solution)/shard_map/ppermute | solution.py:360
  8.5 0.0 collective-permute-start.18
  8.5 0.0 collective-permute-done.11.refs_1_
  8.5 2.6 %collective-permute-start.6 = (bf16[128,1024]{1,0:T(8,128)(2,1)S(1)}, bf16[128,1024]{1,0:T(8,128)(2,1)S(1)}, u32[]{:S(2)}, u32[]{:S(2)}) collective-permute-start(bf16[128,1024]{1,0:T(8,128)(2,1)S(1)} %get-tuple-element.75), channel_id=1, source_target_pairs={{0,24},{4,28},{8,16},{12,20},{16,8},{20,12},{24,0},{28,4},{1,25},{... | collective-permute-start | bytes 786440 | tf_op jit(solution)/shard_map/ppermute | solution.py:360
  11.2 0.7 squeeze.7
  11.9 2.0 %collective-permute-done.15.refs_0_ = bf16[128,1024]{1,0:T(8,128)(2,1)S(1)} collective-permute-done((bf16[128,1024]{1,0:T(8,128)(2,1)S(1)}, bf16[128,1024]{1,0:T(8,128)(2,1)S(1)}, u32[]{:S(2)}, u32[]{:S(2)}) %collective-permute-start.15) | collective-permute-done | bytes 262176 | tf_op jit(solution)/shard_map/ppermute | solution.py:360
  13.9 0.7 collective-permute-start.12
  14.6 4.5 %collective-permute-done.16.refs_1_ = bf16[128,1024]{1,0:T(8,128)(2,1)S(1)} collective-permute-done((bf16[128,1024]{1,0:T(8,128)(2,1)S(1)}, bf16[128,1024]{1,0:T(8,128)(2,1)S(1)}, u32[]{:S(2)}, u32[]{:S(2)}) %collective-permute-start.16) | collective-permute-done | bytes 262176 | tf_op jit(solution)/shard_map/ppermute | solution.py:360
  19.0 0.0 collective-permute-done.17.refs_2_
  19.0 0.0 copy-done.4
  19.1 6.8 %collective-permute-done.18.refs_3_ = bf16[128,1024]{1,0:T(8,128)(2,1)S(1)} collective-permute-done((bf16[128,1024]{1,0:T(8,128)(2,1)S(1)}, bf16[128,1024]{1,0:T(8,128)(2,1)S(1)}, u32[]{:S(2)}, u32[]{:S(2)}) %collective-permute-start.18) | collective-permute-done | bytes 262176 | tf_op jit(solution)/shard_map/ppermute | solution.py:360
  25.9 1.4 %squeeze.8 = (bf16[352,1024]{1,0:T(8,128)(2,1)S(1)}, s32[1,512]{1,0:T(1,128)S(1)}) custom-call(bf16[128,1024]{1,0:T(8,128)(2,1)S(1)} %collective-permute-done.15.refs_0_, bf16[128,1024]{1,0:T(8,128)(2,1)S(1)} %collective-permute-done.16.refs_1_, bf16[128,1024]{1,0:T(8,128)(2,1)S(1)} %collective-permute-done.17.refs_2_, ...), custom_call_target="tpu_custom_call" | custom-call | flops 369098752 | bytes 1769472 | tf_op jit(solution)/shard_map/squeeze/pallas_call | solution.py:107
  27.3 0.0 copy-done.10
  27.3 0.0 copy-done.12
  27.3 0.0 copy-done.14
  27.3 0.0 copy-done.16
  27.3 0.7 collective-permute-start.19
  28.0 0.7 collective-permute-start.20
  28.7 6.1 %collective-permute-start.21 = (bf16[352,1024]{1,0:T(8,128)(2,1)S(1)}, bf16[352,1024]{1,0:T(8,128)(2,1)S(1)}, u32[]{:S(2)}, u32[]{:S(2)}) collective-permute-start(bf16[352,1024]{1,0:T(8,128)(2,1)S(1)} %get-tuple-element.86.refs_0_), channel_id=1, source_target_pairs={{0,2},{7,5},{8,10},{15,13},{16,18},{23,21},{24,26},{31,29}} | collective-permute-start | bytes 2162696 | tf_op jit(solution)/shard_map/ppermute | solution.py:331
  34.8 0.0 collective-permute-done.6.refs_0_
  34.8 0.0 copy-start.6
  34.8 0.7 collective-permute-start.7
  35.5 8.8 %collective-permute-done.7.refs_1_ = bf16[128,1024]{1,0:T(8,128)(2,1)S(1)} collective-permute-done((bf16[128,1024]{1,0:T(8,128)(2,1)S(1)}, bf16[128,1024]{1,0:T(8,128)(2,1)S(1)}, u32[]{:S(2)}, u32[]{:S(2)}) %collective-permute-start.7) | collective-permute-done | bytes 262176 | tf_op jit(solution)/shard_map/ppermute | solution.py:360
  44.3 1.4 %collective-permute-start.13 = (bf16[192,1024]{1,0:T(8,128)(2,1)S(1)}, bf16[192,1024]{1,0:T(8,128)(2,1)}, u32[]{:S(2)}, u32[]{:S(2)}) collective-permute-start(bf16[192,1024]{1,0:T(8,128)(2,1)S(1)} %get-tuple-element.80.refs_0_), channel_id=1, source_target_pairs={{3,2},{4,5},{11,10},{12,13},{19,18},{20,21},{27,26},{28,29}} | collective-permute-start | bytes 1179656 | tf_op jit(solution)/shard_map/ppermute | solution.py:331
  45.7 0.0 collective-permute-done.12.refs_1_
  45.7 0.0 copy-done.6
  45.7 0.0 copy-done.8
  45.7 0.7 copy-done.2
  46.5 2.0 %collective-permute-start.14 = (bf16[192,1024]{1,0:T(8,128)(2,1)S(1)}, bf16[192,1024]{1,0:T(8,128)(2,1)}, u32[]{:S(2)}, u32[]{:S(2)}) collective-permute-start(bf16[192,1024]{1,0:T(8,128)(2,1)S(1)} %get-tuple-element.80.refs_0_), channel_id=1, source_target_pairs={{0,2},{7,5},{8,10},{15,13},{16,18},{23,21},{24,26},{31,29}} | collective-permute-start | bytes 1179656 | tf_op jit(solution)/shard_map/ppermute | solution.py:331
  48.5 1.8 %squeeze.6 = (bf16[192,1024]{1,0:T(8,128)(2,1)S(1)}, s32[1,256]{1,0:T(1,128)S(1)}) custom-call(bf16[128,1024]{1,0:T(8,128)(2,1)} %copy-done.6, bf16[128,1024]{1,0:T(8,128)(2,1)} %copy-done.8), custom_call_target="tpu_custom_call" | custom-call | flops 100663296 | bytes 917504 | tf_op jit(solution)/shard_map/squeeze/pallas_call | solution.py:107
  50.3 0.0 collective-permute-done.13.refs_2_
  50.3 0.7 collective-permute-start.22
  51.0 5.8 %collective-permute-done.14.refs_3_ = bf16[192,1024]{1,0:T(8,128)(2,1)} collective-permute-done((bf16[192,1024]{1,0:T(8,128)(2,1)S(1)}, bf16[192,1024]{1,0:T(8,128)(2,1)}, u32[]{:S(2)}, u32[]{:S(2)}) %collective-permute-start.14) | collective-permute-done | bytes 393248 | tf_op jit(solution)/shard_map/ppermute | solution.py:331
  56.9 0.6 collective-permute-start.23
  57.5 0.0 copy-start.3
  57.5 1.0 copy-done.3
  58.5 1.1 %pair.3 = (bf16[768,1024]{1,0:T(8,128)(2,1)S(1)}, f32[1,768]{1,0:T(1,128)S(1)}, f32[1,768]{1,0:T(1,128)S(1)}) custom-call(s32[1]{0:T(128)} %bitcast.4.owner_ref, bf16[192,1024]{1,0:T(8,128)(2,1)S(1)} %get-tuple-element.80.refs_0_, bf16[192,1024]{1,0:T(8,128)(2,1)S(1)} %copy-done.3, bf16[192,1024]{1,0:T(8,128)(2,1)} %collective-permute-done.13.refs_2_, ...), custom_call_target="tpu_custom_call" | custom-call | flops 603979776 | bytes 1572864 | tf_op jit(solution)/shard_map/pair/pallas_call | solution.py:188
  59.6 0.0 collective-permute-done.19.refs_1_
  59.6 8.9 %collective-permute-start.10 = (bf16[192,1024]{1,0:T(8,128)(2,1)S(1)}, bf16[192,1024]{1,0:T(8,128)(2,1)S(1)}, u32[]{:S(2)}, u32[]{:S(2)}) collective-permute-start(bf16[192,1024]{1,0:T(8,128)(2,1)S(1)} %get-tuple-element.77.refs_0_), channel_id=1, source_target_pairs={{0,2},{7,5},{8,10},{15,13},{16,18},{23,21},{24,26},{31,29}} | collective-permute-start | bytes 1179656 | tf_op jit(solution)/shard_map/ppermute | solution.py:331
  68.5 0.0 collective-permute-done.20.refs_2_
  68.5 0.7 collective-permute-start.8
  69.2 0.0 collective-permute-done.21.refs_3_
  69.2 0.7 collective-permute-start.9
  69.9 7.2 %collective-permute-done.10.refs_3_ = bf16[192,1024]{1,0:T(8,128)(2,1)S(1)} collective-permute-done((bf16[192,1024]{1,0:T(8,128)(2,1)S(1)}, bf16[192,1024]{1,0:T(8,128)(2,1)S(1)}, u32[]{:S(2)}, u32[]{:S(2)}) %collective-permute-start.10) | collective-permute-done | bytes 393248 | tf_op jit(solution)/shard_map/ppermute | solution.py:331
  77.1 5.3 %collective-permute-start.24 = (s32[1,1024]{1,0:T(1,128)S(1)}, s32[1,1024]{1,0:T(1,128)S(1)}, u32[]{:S(2)}, u32[]{:S(2)}) collective-permute-start(s32[1,1024]{1,0:T(1,128)S(1)} %constant_dynamic-update-slice_fusion.refs_3_), channel_id=1, source_target_pairs={{0,2},{7,5},{8,10},{15,13},{16,18},{23,21},{24,26},{31,29}} | collective-permute-start | bytes 12296 | tf_op jit(solution)/shard_map/ppermute | solution.py:341
  82.4 0.0 collective-permute-done.8.refs_1_
  82.4 0.0 collective-permute-done.9.refs_2_
  82.4 0.0 copy-start.5
  82.5 0.0 copy-start.7
  82.5 0.0 copy-start.9
  82.5 1.4 %pair.5 = (bf16[768,1024]{1,0:T(8,128)(2,1)}, f32[1,768]{1,0:T(1,128)}, f32[1,768]{1,0:T(1,128)S(1)}, f32[1,768]{1,0:T(1,128)S(1)}, f32[1,1408]{1,0:T(1,128)S(1)}) custom-call(s32[1]{0:T(128)} %bitcast.4.owner_ref, bf16[192,1024]{1,0:T(8,128)(2,1)S(1)} %get-tuple-element.77.refs_0_, bf16[192,1024]{1,0:T(8,128)(2,1)S(1)} %collective-permute-done.8.refs_1_, ...), custom_call_target="tpu_custom_call" | custom-call | flops 4026531840 | bytes 1572864 | tf_op jit(solution)/shard_map/pair/pallas_call | solution.py:188
  83.9 0.0 collective-permute-done.22.refs_4_
  83.9 0.0 collective-permute-done.23.refs_5_
  83.9 0.0 collective-permute-done.24.refs_6_
  83.9 0.6 spread.3
  84.5 8.2 %all-to-all-start.1 = ((f32[32,1,128]{2,1,0:T(1,128)}), f32[32,1,128]{2,1,0:T(1,128)S(1)}, u32[]{:S(2)}, u32[]{:S(2)}) async-start(f32[32,1,128]{2,1,0:T(1,128)} %spread.3), calls=%async_computation.1 | async-start | bytes 32768 | tf_op jit(solution)/shard_map/all_to_all | solution.py:344
  92.8 7.2 %all-to-all-done.1.got_ref = f32[32,1,128]{2,1,0:T(1,128)S(1)} async-done(((f32[32,1,128]{2,1,0:T(1,128)}), f32[32,1,128]{2,1,0:T(1,128)S(1)}, u32[]{:S(2)}, u32[]{:S(2)}) %all-to-all-start.1) | async-done | bytes 16416 | tf_op jit(solution)/shard_map/all_to_all | solution.py:344
  100.0 1.1 %pick.3 = (f32[1,512]{1,0:T(1,128)}, s32[1]{0:T(128)}) custom-call(s32[1,512]{1,0:T(1,128)S(1)} %get-tuple-element.74.pos_ref, f32[32,1,128]{2,1,0:T(1,128)S(1)} %all-to-all-done.1.got_ref), custom_call_target="tpu_custom_call" | custom-call | tf_op jit(solution)/shard_map/pick/pallas_call | solution.py:299
  (25 shorter events, 0.1 us)
Async XLA Ops:
  0.0 1.2 %copy-start = (bf16[512,1024]{1,0:T(8,128)(2,1)S(1)}, bf16[512,1024]{1,0:T(8,128)(2,1)}, u32[]{:S(2)}) copy-start(bf16[512,1024]{1,0:T(8,128)(2,1)} %embed_ref.1) | copy-start | bytes 3145732
  1.2 0.7 copy-start.1
  3.6 4.9 %collective-permute-start.11 = (bf16[128,1024]{1,0:T(8,128)(2,1)S(1)}, bf16[128,1024]{1,0:T(8,128)(2,1)S(1)}, u32[]{:S(2)}, u32[]{:S(2)}) collective-permute-start(bf16[128,1024]{1,0:T(8,128)(2,1)S(1)} %get-tuple-element.79), channel_id=1, source_target_pairs={{0,4},{4,0},{8,12},{12,8},{16,20},{20,16},{24,28},{28,24},{1,5},{5... | collective-permute-start | bytes 786440 | tf_op jit(solution)/shard_map/ppermute | solution.py:360
  4.2 9.7 %collective-permute-start.15 = (bf16[128,1024]{1,0:T(8,128)(2,1)S(1)}, bf16[128,1024]{1,0:T(8,128)(2,1)S(1)}, u32[]{:S(2)}, u32[]{:S(2)}) collective-permute-start(bf16[128,1024]{1,0:T(8,128)(2,1)S(1)} %get-tuple-element.82), channel_id=1, source_target_pairs={{0,8},{4,12},{8,0},{12,4},{16,24},{20,28},{24,16},{28,20},{1,9},{5... | collective-permute-start | bytes 786440 | tf_op jit(solution)/shard_map/ppermute | solution.py:360
  6.7 12.3 %collective-permute-start.16 = (bf16[128,1024]{1,0:T(8,128)(2,1)S(1)}, bf16[128,1024]{1,0:T(8,128)(2,1)S(1)}, u32[]{:S(2)}, u32[]{:S(2)}) collective-permute-start(bf16[128,1024]{1,0:T(8,128)(2,1)S(1)} %get-tuple-element.83), channel_id=1, source_target_pairs={{0,12},{4,8},{8,4},{12,0},{16,28},{20,24},{24,20},{28,16},{1,13},{... | collective-permute-start | bytes 786440 | tf_op jit(solution)/shard_map/ppermute | solution.py:360
  6.8 12.3 %collective-permute-start.17 = (bf16[128,1024]{1,0:T(8,128)(2,1)S(1)}, bf16[128,1024]{1,0:T(8,128)(2,1)S(1)}, u32[]{:S(2)}, u32[]{:S(2)}) collective-permute-start(bf16[128,1024]{1,0:T(8,128)(2,1)S(1)} %get-tuple-element.84), channel_id=1, source_target_pairs={{0,16},{4,20},{8,24},{12,28},{16,0},{20,4},{24,8},{28,12},{1,17},{... | collective-permute-start | bytes 786440 | tf_op jit(solution)/shard_map/ppermute | solution.py:360
  8.5 17.3 %collective-permute-start.18 = (bf16[128,1024]{1,0:T(8,128)(2,1)S(1)}, bf16[128,1024]{1,0:T(8,128)(2,1)S(1)}, u32[]{:S(2)}, u32[]{:S(2)}) collective-permute-start(bf16[128,1024]{1,0:T(8,128)(2,1)S(1)} %get-tuple-element.85), channel_id=1, source_target_pairs={{0,20},{4,16},{8,28},{12,24},{16,4},{20,0},{24,12},{28,8},{1,21},{... | collective-permute-start | bytes 786440 | tf_op jit(solution)/shard_map/ppermute | solution.py:360
  8.5 10.5 %copy-start.4 = (bf16[128,1024]{1,0:T(8,128)(2,1)}, bf16[128,1024]{1,0:T(8,128)(2,1)S(1)}, u32[]{:S(2)}) copy-start(bf16[128,1024]{1,0:T(8,128)(2,1)S(1)} %collective-permute-done.11.refs_1_) | copy-start | bytes 786436
  8.5 26.3 %collective-permute-start.6 = (bf16[128,1024]{1,0:T(8,128)(2,1)S(1)}, bf16[128,1024]{1,0:T(8,128)(2,1)S(1)}, u32[]{:S(2)}, u32[]{:S(2)}) collective-permute-start(bf16[128,1024]{1,0:T(8,128)(2,1)S(1)} %get-tuple-element.75), channel_id=1, source_target_pairs={{0,24},{4,28},{8,16},{12,20},{16,8},{20,12},{24,0},{28,4},{1,25},{... | collective-permute-start | bytes 786440 | tf_op jit(solution)/shard_map/ppermute | solution.py:360
  13.9 13.4 %copy-start.10 = (bf16[128,1024]{1,0:T(8,128)(2,1)}, bf16[128,1024]{1,0:T(8,128)(2,1)S(1)}, u32[]{:S(2)}) copy-start(bf16[128,1024]{1,0:T(8,128)(2,1)S(1)} %collective-permute-done.15.refs_0_) | copy-start | bytes 786436
  13.9 31.8 %collective-permute-start.12 = (bf16[192,1024]{1,0:T(8,128)(2,1)S(1)}, bf16[192,1024]{1,0:T(8,128)(2,1)S(1)}, u32[]{:S(2)}, u32[]{:S(2)}) collective-permute-start(bf16[192,1024]{1,0:T(8,128)(2,1)S(1)} %get-tuple-element.80.refs_0_), channel_id=1, source_target_pairs={{1,2},{6,5},{9,10},{14,13},{17,18},{22,21},{25,26},{30,29}} | collective-permute-start | bytes 1179656 | tf_op jit(solution)/shard_map/ppermute | solution.py:331
  19.0 8.2 %copy-start.12 = (bf16[128,1024]{1,0:T(8,128)(2,1)}, bf16[128,1024]{1,0:T(8,128)(2,1)S(1)}, u32[]{:S(2)}) copy-start(bf16[128,1024]{1,0:T(8,128)(2,1)S(1)} %collective-permute-done.16.refs_1_) | copy-start | bytes 786436
  19.0 8.2 %copy-start.14 = (bf16[128,1024]{1,0:T(8,128)(2,1)}, bf16[128,1024]{1,0:T(8,128)(2,1)S(1)}, u32[]{:S(2)}) copy-start(bf16[128,1024]{1,0:T(8,128)(2,1)S(1)} %collective-permute-done.17.refs_2_) | copy-start | bytes 786436
  25.9 1.4 %copy-start.16 = (bf16[128,1024]{1,0:T(8,128)(2,1)}, bf16[128,1024]{1,0:T(8,128)(2,1)S(1)}, u32[]{:S(2)}) copy-start(bf16[128,1024]{1,0:T(8,128)(2,1)S(1)} %collective-permute-done.18.refs_3_) | copy-start | bytes 786436
  27.3 32.3 %collective-permute-start.19 = (bf16[352,1024]{1,0:T(8,128)(2,1)S(1)}, bf16[352,1024]{1,0:T(8,128)(2,1)S(1)}, u32[]{:S(2)}, u32[]{:S(2)}) collective-permute-start(bf16[352,1024]{1,0:T(8,128)(2,1)S(1)} %get-tuple-element.86.refs_0_), channel_id=1, source_target_pairs={{1,2},{6,5},{9,10},{14,13},{17,18},{22,21},{25,26},{30,29}} | collective-permute-start | bytes 2162696 | tf_op jit(solution)/shard_map/ppermute | solution.py:331
  28.0 40.5 %collective-permute-start.20 = (bf16[352,1024]{1,0:T(8,128)(2,1)S(1)}, bf16[352,1024]{1,0:T(8,128)(2,1)S(1)}, u32[]{:S(2)}, u32[]{:S(2)}) collective-permute-start(bf16[352,1024]{1,0:T(8,128)(2,1)S(1)} %get-tuple-element.86.refs_0_), channel_id=1, source_target_pairs={{3,2},{4,5},{11,10},{12,13},{19,18},{20,21},{27,26},{28,29}} | collective-permute-start | bytes 2162696 | tf_op jit(solution)/shard_map/ppermute | solution.py:331
  28.7 40.5 %collective-permute-start.21 = (bf16[352,1024]{1,0:T(8,128)(2,1)S(1)}, bf16[352,1024]{1,0:T(8,128)(2,1)S(1)}, u32[]{:S(2)}, u32[]{:S(2)}) collective-permute-start(bf16[352,1024]{1,0:T(8,128)(2,1)S(1)} %get-tuple-element.86.refs_0_), channel_id=1, source_target_pairs={{0,2},{7,5},{8,10},{15,13},{16,18},{23,21},{24,26},{31,29}} | collective-permute-start | bytes 2162696 | tf_op jit(solution)/shard_map/ppermute | solution.py:331
  34.8 10.9 %copy-start.6 = (bf16[128,1024]{1,0:T(8,128)(2,1)}, bf16[128,1024]{1,0:T(8,128)(2,1)S(1)}, u32[]{:S(2)}) copy-start(bf16[128,1024]{1,0:T(8,128)(2,1)S(1)} %collective-permute-done.6.refs_0_) | copy-start | bytes 786436
  34.8 9.5 %collective-permute-start.7 = (bf16[128,1024]{1,0:T(8,128)(2,1)S(1)}, bf16[128,1024]{1,0:T(8,128)(2,1)S(1)}, u32[]{:S(2)}, u32[]{:S(2)}) collective-permute-start(bf16[128,1024]{1,0:T(8,128)(2,1)S(1)} %get-tuple-element.76), channel_id=1, source_target_pairs={{0,28},{4,24},{8,20},{12,16},{16,12},{20,8},{24,4},{28,0},{1,29},{... | collective-permute-start | bytes 786440 | tf_op jit(solution)/shard_map/ppermute | solution.py:360
  44.3 1.4 %copy-start.8 = (bf16[128,1024]{1,0:T(8,128)(2,1)}, bf16[128,1024]{1,0:T(8,128)(2,1)S(1)}, u32[]{:S(2)}) copy-start(bf16[128,1024]{1,0:T(8,128)(2,1)S(1)} %collective-permute-done.7.refs_1_) | copy-start | bytes 786436
  44.3 6.0 %collective-permute-start.13 = (bf16[192,1024]{1,0:T(8,128)(2,1)S(1)}, bf16[192,1024]{1,0:T(8,128)(2,1)}, u32[]{:S(2)}, u32[]{:S(2)}) collective-permute-start(bf16[192,1024]{1,0:T(8,128)(2,1)S(1)} %get-tuple-element.80.refs_0_), channel_id=1, source_target_pairs={{3,2},{4,5},{11,10},{12,13},{19,18},{20,21},{27,26},{28,29}} | collective-permute-start | bytes 1179656 | tf_op jit(solution)/shard_map/ppermute | solution.py:331
  45.7 0.8 copy-start.2
  46.5 10.4 %collective-permute-start.14 = (bf16[192,1024]{1,0:T(8,128)(2,1)S(1)}, bf16[192,1024]{1,0:T(8,128)(2,1)}, u32[]{:S(2)}, u32[]{:S(2)}) collective-permute-start(bf16[192,1024]{1,0:T(8,128)(2,1)S(1)} %get-tuple-element.80.refs_0_), channel_id=1, source_target_pairs={{0,2},{7,5},{8,10},{15,13},{16,18},{23,21},{24,26},{31,29}} | collective-permute-start | bytes 1179656 | tf_op jit(solution)/shard_map/ppermute | solution.py:331
  50.3 33.5 %collective-permute-start.22 = (s32[1,1024]{1,0:T(1,128)S(1)}, s32[1,1024]{1,0:T(1,128)S(1)}, u32[]{:S(2)}, u32[]{:S(2)}) collective-permute-start(s32[1,1024]{1,0:T(1,128)S(1)} %constant_dynamic-update-slice_fusion.refs_3_), channel_id=1, source_target_pairs={{1,2},{6,5},{9,10},{14,13},{17,18},{22,21},{25,26},{30,29}} | collective-permute-start | bytes 12296 | tf_op jit(solution)/shard_map/ppermute | solution.py:341
  56.9 27.0 %collective-permute-start.23 = (s32[1,1024]{1,0:T(1,128)S(1)}, s32[1,1024]{1,0:T(1,128)S(1)}, u32[]{:S(2)}, u32[]{:S(2)}) collective-permute-start(s32[1,1024]{1,0:T(1,128)S(1)} %constant_dynamic-update-slice_fusion.refs_3_), channel_id=1, source_target_pairs={{3,2},{4,5},{11,10},{12,13},{19,18},{20,21},{27,26},{28,29}} | collective-permute-start | bytes 12296 | tf_op jit(solution)/shard_map/ppermute | solution.py:341
  57.5 1.0 copy-start.3
  59.6 17.5 %collective-permute-start.10 = (bf16[192,1024]{1,0:T(8,128)(2,1)S(1)}, bf16[192,1024]{1,0:T(8,128)(2,1)S(1)}, u32[]{:S(2)}, u32[]{:S(2)}) collective-permute-start(bf16[192,1024]{1,0:T(8,128)(2,1)S(1)} %get-tuple-element.77.refs_0_), channel_id=1, source_target_pairs={{0,2},{7,5},{8,10},{15,13},{16,18},{23,21},{24,26},{31,29}} | collective-permute-start | bytes 1179656 | tf_op jit(solution)/shard_map/ppermute | solution.py:331
  68.5 13.9 %collective-permute-start.8 = (bf16[192,1024]{1,0:T(8,128)(2,1)S(1)}, bf16[192,1024]{1,0:T(8,128)(2,1)S(1)}, u32[]{:S(2)}, u32[]{:S(2)}) collective-permute-start(bf16[192,1024]{1,0:T(8,128)(2,1)S(1)} %get-tuple-element.77.refs_0_), channel_id=1, source_target_pairs={{1,2},{6,5},{9,10},{14,13},{17,18},{22,21},{25,26},{30,29}} | collective-permute-start | bytes 1179656 | tf_op jit(solution)/shard_map/ppermute | solution.py:331
  69.2 13.2 %collective-permute-start.9 = (bf16[192,1024]{1,0:T(8,128)(2,1)S(1)}, bf16[192,1024]{1,0:T(8,128)(2,1)S(1)}, u32[]{:S(2)}, u32[]{:S(2)}) collective-permute-start(bf16[192,1024]{1,0:T(8,128)(2,1)S(1)} %get-tuple-element.77.refs_0_), channel_id=1, source_target_pairs={{3,2},{4,5},{11,10},{12,13},{19,18},{20,21},{27,26},{28,29}} | collective-permute-start | bytes 1179656 | tf_op jit(solution)/shard_map/ppermute | solution.py:331
  77.1 6.8 %collective-permute-start.24 = (s32[1,1024]{1,0:T(1,128)S(1)}, s32[1,1024]{1,0:T(1,128)S(1)}, u32[]{:S(2)}, u32[]{:S(2)}) collective-permute-start(s32[1,1024]{1,0:T(1,128)S(1)} %constant_dynamic-update-slice_fusion.refs_3_), channel_id=1, source_target_pairs={{0,2},{7,5},{8,10},{15,13},{16,18},{23,21},{24,26},{31,29}} | collective-permute-start | bytes 12296 | tf_op jit(solution)/shard_map/ppermute | solution.py:341
  82.4 19.2 %copy-start.5 = (bf16[128,1024]{1,0:T(8,128)(2,1)S(1)}, bf16[128,1024]{1,0:T(8,128)(2,1)}, u32[]{:S(2)}) copy-start(bf16[128,1024]{1,0:T(8,128)(2,1)} %copy-done.4) | copy-start | bytes 786436
  82.5 19.2 %copy-start.7 = (bf16[128,1024]{1,0:T(8,128)(2,1)S(1)}, bf16[128,1024]{1,0:T(8,128)(2,1)}, u32[]{:S(2)}) copy-start(bf16[128,1024]{1,0:T(8,128)(2,1)} %copy-done.6) | copy-start | bytes 786436
  82.5 19.2 %copy-start.9 = (bf16[128,1024]{1,0:T(8,128)(2,1)S(1)}, bf16[128,1024]{1,0:T(8,128)(2,1)}, u32[]{:S(2)}) copy-start(bf16[128,1024]{1,0:T(8,128)(2,1)} %copy-done.8) | copy-start | bytes 786436
  82.5 19.2 %copy-start.11 = (bf16[128,1024]{1,0:T(8,128)(2,1)S(1)}, bf16[128,1024]{1,0:T(8,128)(2,1)}, u32[]{:S(2)}) copy-start(bf16[128,1024]{1,0:T(8,128)(2,1)} %copy-done.10) | copy-start | bytes 786436
  82.5 19.2 %copy-start.13 = (bf16[128,1024]{1,0:T(8,128)(2,1)S(1)}, bf16[128,1024]{1,0:T(8,128)(2,1)}, u32[]{:S(2)}) copy-start(bf16[128,1024]{1,0:T(8,128)(2,1)} %copy-done.12) | copy-start | bytes 786436
  82.5 19.2 %copy-start.15 = (bf16[128,1024]{1,0:T(8,128)(2,1)S(1)}, bf16[128,1024]{1,0:T(8,128)(2,1)}, u32[]{:S(2)}) copy-start(bf16[128,1024]{1,0:T(8,128)(2,1)} %copy-done.14) | copy-start | bytes 786436
  82.5 19.2 %copy-start.17 = (bf16[128,1024]{1,0:T(8,128)(2,1)S(1)}, bf16[128,1024]{1,0:T(8,128)(2,1)}, u32[]{:S(2)}) copy-start(bf16[128,1024]{1,0:T(8,128)(2,1)} %copy-done.16) | copy-start | bytes 786436
  84.5 15.4 %all-to-all-start.1 = ((f32[32,1,128]{2,1,0:T(1,128)}), f32[32,1,128]{2,1,0:T(1,128)S(1)}, u32[]{:S(2)}, u32[]{:S(2)}) async-start(f32[32,1,128]{2,1,0:T(1,128)} %spread.3), calls=%async_computation.1 | async-start | bytes 32768 | tf_op jit(solution)/shard_map/all_to_all | solution.py:344
where the time goes:
time: 102 us
  starting transfers between devices  44.9 us (44%)
  waiting for transfers between devices  42.3 us (41%)
  Pallas kernels  9.79 us (10%)
  local copies, waits for them, and re-layouts  3.72 us (4%)
  between operations  1.16 us (1%)
    ppermute x7, waiting for transfers between devices, on_device(): held.append(lax.ppermute(sent[k], 'grp', xor(nsec, k)))  22.1 us
    ppermute x9, starting transfers between devices, best_of_all(): blocks.append(lax.ppermute(group, AXES, route))  21.9 us
    ppermute x9, waiting for transfers between devices, best_of_all(): blocks.append(lax.ppermute(group, AXES, route))  13.1 us
    all_to_all x1, starting transfers between devices, best_of_all(): lax.all_to_all(sorted_out, AXES, split_axis=0, concat_axis=0, tiled=True)  8.22 us
    ppermute x7, starting transfers between devices, on_device(): held.append(lax.ppermute(sent[k], 'grp', xor(nsec, k)))  8.22 us
    all_to_all x1, waiting for transfers between devices, best_of_all(): lax.all_to_all(sorted_out, AXES, split_axis=0, concat_axis=0, tiled=True)  7.2 us
    ppermute x3, starting transfers between devices, best_of_all(): spots.append(lax.ppermute(place, AXES, route))  6.58 us
    pallas_call x3, Pallas kernels, squeeze(): pl.pallas_call(functools.partial(squeeze_kernel, len(sections)), out_shap...  3.89 us
  transfers between devices with their start and end apart: 20, of which 7 were waited for; matrix products, arithmetic and copies ran while one was open for 0% of the time, Pallas kernels for 6%

commit v1 on v0

--- a/solution.py
+++ b/solution.py
@@ -20,43 +20,57 @@
 TILE = 256
 
 
-def pack_kernel(nsec, cap, nblk, me_ref, dest_ref, embed_ref, *outs):
-    pos_ref, sections = outs[0], outs[1:]
+def pack_kernel(nsec, cap, stride, nblk, me_ref, dest_hbm, embed_hbm, *refs):
+    pos_ref, sections = refs[0], refs[1 : nsec + 1]
+    dest_ref, embed_ref, dest_sem, embed_sem = refs[nsec + 1 :]
+    dest_copy = pltpu.make_async_copy(dest_hbm, dest_ref, dest_sem)
+    embed_copy = pltpu.make_async_copy(embed_hbm, embed_ref, embed_sem)
+    dest_copy.start()
+    embed_copy.start()
     count = embed_ref.shape[0]
+    lower = lax.broadcasted_iota(jnp.int32, (count, count), 0) < lax.broadcasted_iota(
+        jnp.int32, (count, count), 1
+    )
+    lower = lower.astype(F32).astype(BF16)
+    dest_copy.wait()
     cluster = lax.div(dest_ref[...], nblk)
     part = cluster ^ me_ref[0]
     onehot = lax.broadcasted_iota(jnp.int32, (nsec, count), 0) == part
-    lower = lax.broadcasted_iota(jnp.int32, (count, count), 0) < lax.broadcasted_iota(
-        jnp.int32, (count, count), 1
-    )
-    before = jnp.dot(
-        onehot.astype(F32).astype(BF16), lower.astype(F32).astype(BF16), preferred_element_type=F32
-    )
+    before = jnp.dot(onehot.astype(F32).astype(BF16), lower, preferred_element_type=F32)
     rank = jnp.sum(jnp.where(onehot, before, 0.0), axis=0, keepdims=True).astype(jnp.int32)
-    pos = part * cap + rank
-    pos_ref[...] = cluster * cap + rank
-    wide = embed_ref[...].astype(F32)
-    unit = (wide * lax.rsqrt(jnp.sum(wide * wide, axis=1, keepdims=True) + 1e-06)).astype(BF16)
+    pos_ref[...] = jnp.where(rank < cap, cluster * stride + rank, -1)
+    pos = jnp.where(rank < cap, part * cap + rank, -1)
     held = jnp.sum(onehot.astype(F32), axis=1, keepdims=True)
     rows = lax.broadcasted_iota(jnp.int32, (cap, 128), 0).astype(F32)
     first = lax.broadcasted_iota(jnp.int32, (cap, 128), 1) == 0
+    embed_copy.wait()
+    wide = embed_ref[...].astype(F32)
+    unit = (wide * lax.rsqrt(jnp.sum(wide * wide, axis=1, keepdims=True) + 1e-06)).astype(BF16)
     for k, out in enumerate(sections):
         pick = lax.broadcasted_iota(jnp.int32, (cap, count), 0) + k * cap == pos
-        out[...] = jnp.dot(
-            pick.astype(F32).astype(BF16), unit, preferred_element_type=F32
-        ).astype(BF16)
-        mark = jnp.where(first & (rows >= held[k : k + 1, :]), PAD, 0.0)
-        out[:, 0:128] = (out[:, 0:128].astype(F32) + mark).astype(BF16)
-
-
-def pack(embed, dest, me, nsec, cap, nblk):
+        value = jnp.dot(pick.astype(F32).astype(BF16), unit, preferred_element_type=F32)
+        out[...] = value.astype(BF16)
+        many = held[k : k + 1, :]
+        head = jnp.where(first & (rows >= many), PAD, value[:, 0:128])
+        head = jnp.where(first & (rows == cap - 1.0) & (many > cap), FULL, head)
+        out[:, 0:128] = head.astype(BF16)
+
+
+def pack(embed, dest, me, nsec, cap, stride, nblk):
     count, width = embed.shape
-    return pl.pallas_call(
-        functools.partial(pack_kernel, nsec, cap, nblk),
+    hbm = pl.BlockSpec(memory_space=pltpu.HBM)
+    return pl.pallas_call(
+        functools.partial(pack_kernel, nsec, cap, stride, nblk),
         out_shape=[jax.ShapeDtypeStruct((1, count), jnp.int32)]
         + [jax.ShapeDtypeStruct((cap, width), BF16)] * nsec,
-        in_specs=[SMEM, VMEM, VMEM],
+        in_specs=[SMEM, hbm, hbm],
         out_specs=[VMEM] * (nsec + 1),
+        scratch_shapes=[
+            pltpu.VMEM((1, count), jnp.int32),
+            pltpu.VMEM((count, width), BF16),
+            pltpu.SemaphoreType.DMA,
+            pltpu.SemaphoreType.DMA,
+        ],
         compiler_params=pltpu.CompilerParams(vmem_limit_bytes=24 << 20),
         name="pack",
     )(me, dest.reshape(1, count), embed)
@@ -71,12 +85,19 @@
     return scores(first.astype(F32).astype(BF16), rows_ref[...])[0:1, :]
 
 
-def squeeze_kernel(nsec, *refs):
-    sections, out_ref, pos_ref = refs[:nsec], refs[nsec], refs[nsec + 1]
+def squeeze_kernel(nsec, stride, *refs):
+    sections, out_ref, pos_ref, all_ref = refs[:nsec], refs[nsec], refs[nsec + 1], refs[nsec + 2]
     room = out_ref.shape[0]
     cap = sections[0].shape[0]
-    size = nsec * cap
-    filled = jnp.concatenate([first_entries(s) for s in sections], axis=1) < 1.5
+    size = nsec * stride
+    for k, section in enumerate(sections):
+        all_ref[k * stride : k * stride + cap, :] = section[...]
+        if cap < stride:
+            all_ref[k * stride + cap : (k + 1) * stride, :] = jnp.full(
+                (stride - cap, all_ref.shape[1]), PAD, BF16
+            )
+    entries = first_entries(all_ref)
+    filled = entries < 1.5
     lower = lax.broadcasted_iota(jnp.int32, (size, size), 0) < lax.broadcasted_iota(
         jnp.int32, (size, size), 1
     )
@@ -85,34 +106,32 @@
         ones.astype(BF16), lower.astype(F32).astype(BF16), preferred_element_type=F32
     )[0:1, :]
     total = jnp.sum(filled.astype(F32), axis=1, keepdims=True)
+    left_out = (total > room) | (jnp.max(entries, axis=1, keepdims=True) > 3.0)
     pos = jnp.where(filled, before, -1.0).astype(jnp.int32)
     pos_ref[...] = pos
     pick = (lax.broadcasted_iota(jnp.int32, (room, size), 0) == pos).astype(F32).astype(BF16)
-    value = jnp.dot(pick[:, 0:cap], sections[0][...], preferred_element_type=F32)
-    for k in range(1, nsec):
-        value = value + jnp.dot(
-            pick[:, k * cap : (k + 1) * cap], sections[k][...], preferred_element_type=F32
-        )
+    value = jnp.dot(pick, all_ref[...], preferred_element_type=F32)
     out_ref[...] = value.astype(BF16)
     rows = lax.broadcasted_iota(jnp.int32, (room, 128), 0).astype(F32)
     first = lax.broadcasted_iota(jnp.int32, (room, 128), 1) == 0
     head = jnp.where(first & (rows >= total), PAD, value[:, 0:128])
-    head = jnp.where(first & (rows == room - 1.0) & (total > room), FULL, head)
+    head = jnp.where(first & (rows == room - 1.0) & left_out, FULL, head)
     out_ref[:, 0:128] = head.astype(BF16)
 
 
-def squeeze(sections, room):
-    cap, width = sections[0].shape
-    size = len(sections) * cap
-    return pl.pallas_call(
-        functools.partial(squeeze_kernel, len(sections)),
+def squeeze(sections, room, stride):
+    width = sections[0].shape[1]
+    size = len(sections) * stride
+    return pl.pallas_call(
+        functools.partial(squeeze_kernel, len(sections), stride),
         out_shape=[
             jax.ShapeDtypeStruct((room, width), BF16),
             jax.ShapeDtypeStruct((1, size), jnp.int32),
         ],
         in_specs=[VMEM] * len(sections),
         out_specs=[VMEM] * 2,
-        compiler_params=pltpu.CompilerParams(vmem_limit_bytes=12 << 20),
+        scratch_shapes=[pltpu.VMEM((size, width), BF16)],
+        compiler_params=pltpu.CompilerParams(vmem_limit_bytes=16 << 20),
         cost_estimate=pl.CostEstimate(
             flops=2 * room * size * width, bytes_accessed=2 * (room + size) * width, transcendentals=0
         ),
@@ -150,10 +169,11 @@
         col_best = []
         for lo, tile in tiles(rows):
             value = scores(new_ref[lo:, :], new_ref[lo : lo + tile, :])
-            same = lax.broadcasted_iota(jnp.int32, value.shape, 0) == lax.broadcasted_iota(
-                jnp.int32, value.shape, 1
+            same = lax.broadcasted_iota(jnp.int32, (tile, tile), 0) == lax.broadcasted_iota(
+                jnp.int32, (tile, tile), 1
             )
-            value = jnp.where(same, LOW, value)
+            head = jnp.where(same, LOW, value[0:tile])
+            value = jnp.concatenate([head, value[tile:]], axis=0) if tile < rows - lo else head
             fold(lo, value + bias_ref[:, lo : lo + tile])
             col_best.append(jnp.max(value + down[lo:, :], axis=0, keepdims=True))
         for old, bias, best, out in zip(olds, bias_olds, best_olds, best_outs):
@@ -313,8 +333,11 @@
     return [(g, g ^ bits) for g in range(nsec)]
 
 
-def best_of_all(held, owner, me, pos, parts, share, nblk):
-    nsec, cap = len(held), held[0].shape[0]
+def best_of_all(embed, dest, owner, me, cap, stride, parts, rooms, nsec, nblk):
+    pos, *sent = pack(embed, dest, me, nsec, cap, stride, nblk)
+    held = [sent[0]]
+    for k in range(1, nsec):
+        held.append(lax.ppermute(sent[k], "grp", xor(nsec, k)))
     upper = nblk // 2
     order = sorted((z for z in range(nblk) if z != upper), key=lambda z: abs(z - upper))
     flip = lambda b, core: b if core == 0 else nblk - 1 - b
@@ -324,7 +347,7 @@
     ]
     arrays, biases, bests, places = [], [], [], []
     for q, (lo, hi) in enumerate(parts):
-        group, place = squeeze(held[lo:hi], share[q] * (hi - lo) * cap // 16)
+        group, place = squeeze(held[lo:hi], rooms[q], stride)
         places.append(place)
         blocks = [group]
         for route in routes:
@@ -340,7 +363,7 @@
     for route in routes:
         spots.append(lax.ppermute(place, AXES, route))
     counts = tuple(hi - lo for lo, hi in parts)
-    sorted_out = spread(owner, me, bests, spots, counts, (upper, *order), nsec, cap)
+    sorted_out = spread(owner, me, bests, spots, counts, (upper, *order), nsec, stride)
     got = lax.all_to_all(sorted_out, AXES, split_axis=0, concat_axis=0, tiled=True)
     return pick(pos, got, nsec, nblk)
 
@@ -352,16 +375,15 @@
     grp, blk = lax.axis_index("grp"), lax.axis_index("blk")
     me = grp.astype(jnp.int32).reshape(1)
     owner = (blk == nblk // 2 - grp % 2).astype(jnp.int32).reshape(1)
-    pos, *sent = pack(embed, dest, me, nsec, cap, nblk)
     quarter = nsec // 4
     parts = [(0, quarter), (quarter, 3 * quarter), (3 * quarter, nsec)]
-    held = [sent[0]]
-    for k in range(1, nsec):
-        held.append(lax.ppermute(sent[k], "grp", xor(nsec, k)))
-    best, redo = best_of_all(held, owner, me, pos, parts, (12, 11, 12), nblk)
+    rooms = [3 * quarter * cap // 4, 11 * quarter * cap // 8, 3 * quarter * cap // 4]
+    best, redo = best_of_all(embed, dest, owner, me, 7 * cap // 8, cap, parts, rooms, nsec, nblk)
     best = lax.cond(
         redo[0] > 0,
-        lambda: best_of_all(held, owner, me, pos, [(0, nsec)], (16,), nblk)[0],
+        lambda: best_of_all(
+            embed, dest, owner, me, cap, cap, [(0, nsec)], [nsec * cap], nsec, nblk
+        )[0],
         lambda: best,
     )
     return best.reshape(count)

time: 102 us -> 95.4 us (0.935)
  waiting for transfers between devices: 42.3 us -> 33.2 us
  starting transfers between devices: 44.9 us -> 48.3 us
  local copies, waits for them, and re-layouts: 3.72 us -> 1.8 us
    ppermute x9, waiting for transfers between devices: 13.1 us -> 7.58 us  [best_of_all(): blocks.append(lax.ppermute(group, AXES, route))]
    ppermute x7, waiting for transfers between devices: 22.1 us -> 18.4 us  [best_of_all(): held.append(lax.ppermute(sent[k], 'grp', xor(nsec, k)))]
    ppermute x3, starting transfers between devices: 6.58 us -> 10.1 us  [best_of_all(): spots.append(lax.ppermute(place, AXES, route))]
    unnamed x38 -> x10, local copies, waits for them, and re-layouts: 3.71 us -> 1.79 us
  transfers between devices with their start and end apart: 20 -> 20, of which waited for: 7 -> 6; matrix products, arithmetic and copies ran while one was open for 0% -> 0% of each run, Pallas kernels for 6% -> 6%
where the time goes in v1:
time: 95.4 us; the launch traced here: 94.9 us
  starting transfers between devices  48.3 us (51%)
  waiting for transfers between devices  33.2 us (35%)
  Pallas kernels  10.6 us (11%)
  local copies, waits for them, and re-layouts  1.8 us (2%)
  between operations  1.03 us (1%)
    ppermute x9, starting transfers between devices, best_of_all(): blocks.append(lax.ppermute(group, AXES, route))  21.7 us
    ppermute x7, waiting for transfers between devices, best_of_all(): held.append(lax.ppermute(sent[k], 'grp', xor(nsec, k)))  18.4 us
    ppermute x3, starting transfers between devices, best_of_all(): spots.append(lax.ppermute(place, AXES, route))  10.1 us
    all_to_all x1, starting transfers between devices, best_of_all(): lax.all_to_all(sorted_out, AXES, split_axis=0, concat_axis=0, tiled=True)  8.24 us
    ppermute x7, starting transfers between devices, best_of_all(): held.append(lax.ppermute(sent[k], 'grp', xor(nsec, k)))  8.22 us
    ppermute x9, waiting for transfers between devices, best_of_all(): blocks.append(lax.ppermute(group, AXES, route))  7.58 us
    all_to_all x1, waiting for transfers between devices, best_of_all(): lax.all_to_all(sorted_out, AXES, split_axis=0, concat_axis=0, tiled=True)  7.19 us
    pallas_call x3, Pallas kernels, squeeze(): pl.pallas_call(functools.partial(squeeze_kernel, len(sections), stride),...  3.42 us
  transfers between devices with their start and end apart: 20, of which 6 were waited for; matrix products, arithmetic and copies ran while one was open for 0% of the time, Pallas kernels for 6%

profile of v1, /device:TPU:0, one launch (start us, length us, event | category | flops | bytes accessed | tf_op | source)
XLA Modules:
  0.0 94.9 jit_solution(8825276454376380894)
XLA Ops:
  0.0 2.9 %pack.3 = (s32[1,512]{1,0:T(1,128)S(1)}, bf16[112,1024]{1,0:T(8,128)(2,1)S(1)}, bf16[112,1024]{1,0:T(8,128)(2,1)S(1)}, bf16[112,1024]{1,0:T(8,128)(2,1)S(1)}, bf...) custom-call(s32[1]{0:T(128)} %bitcast.3.me_ref, ...), custom_call_target="tpu_custom_call" | custom-call | tf_op jit(solution)/shard_map/pack/pallas_call | solution.py:62
  2.9 0.6 collective-permute-start.18
  3.5 2.5 %collective-permute-start.22 = (bf16[112,1024]{1,0:T(8,128)(2,1)S(1)}, bf16[112,1024]{1,0:T(8,128)(2,1)S(1)}, u32[]{:S(2)}, u32[]{:S(2)}) collective-permute-start(bf16[112,1024]{1,0:T(8,128)(2,1)S(1)} %get-tuple-element.70), channel_id=1, source_target_pairs={{0,8},{4,12},{8,0},{12,4},{16,24},{20,28},{24,16},{28,20},{1,9},{5... | collective-permute-start | bytes 688136 | tf_op jit(solution)/shard_map/ppermute | solution.py:340
  6.0 0.0 collective-permute-start.23
  6.0 1.8 %collective-permute-start.24 = (bf16[112,1024]{1,0:T(8,128)(2,1)S(1)}, bf16[112,1024]{1,0:T(8,128)(2,1)S(1)}, u32[]{:S(2)}, u32[]{:S(2)}) collective-permute-start(bf16[112,1024]{1,0:T(8,128)(2,1)S(1)} %get-tuple-element.72), channel_id=1, source_target_pairs={{0,16},{4,20},{8,24},{12,28},{16,0},{20,4},{24,8},{28,12},{1,17},{... | collective-permute-start | bytes 688136 | tf_op jit(solution)/shard_map/ppermute | solution.py:340
  7.8 0.0 collective-permute-start.25
  7.8 0.0 collective-permute-done.18.refs_1_
  7.8 2.6 %collective-permute-start.13 = (bf16[112,1024]{1,0:T(8,128)(2,1)S(1)}, bf16[112,1024]{1,0:T(8,128)(2,1)S(1)}, u32[]{:S(2)}, u32[]{:S(2)}) collective-permute-start(bf16[112,1024]{1,0:T(8,128)(2,1)S(1)} %get-tuple-element.63), channel_id=1, source_target_pairs={{0,24},{4,28},{8,16},{12,20},{16,8},{20,12},{24,0},{28,4},{1,25},{... | collective-permute-start | bytes 688136 | tf_op jit(solution)/shard_map/ppermute | solution.py:340
  10.5 1.6 %squeeze.7 = (bf16[192,1024]{1,0:T(8,128)(2,1)}, s32[1,256]{1,0:T(1,128)S(1)}) custom-call(bf16[112,1024]{1,0:T(8,128)(2,1)S(1)} %get-tuple-element.66.refs_0_, bf16[112,1024]{1,0:T(8,128)(2,1)S(1)} %collective-permute-done.18.refs_1_), custom_call_target="tpu_custom_call" | custom-call | flops 100663296 | bytes 917504 | tf_op jit(solution)/shard_map/squeeze/pallas_call | solution.py:125
  12.0 0.4 collective-permute-done.22.refs_0_
  12.5 0.7 collective-permute-start.19
  13.1 3.8 %collective-permute-done.23.refs_1_ = bf16[112,1024]{1,0:T(8,128)(2,1)S(1)} collective-permute-done((bf16[112,1024]{1,0:T(8,128)(2,1)S(1)}, bf16[112,1024]{1,0:T(8,128)(2,1)S(1)}, u32[]{:S(2)}, u32[]{:S(2)}) %collective-permute-start.23) | collective-permute-done | bytes 229408 | tf_op jit(solution)/shard_map/ppermute | solution.py:340
  16.9 0.0 collective-permute-done.24.refs_2_
  16.9 6.1 %collective-permute-done.25.refs_3_ = bf16[112,1024]{1,0:T(8,128)(2,1)S(1)} collective-permute-done((bf16[112,1024]{1,0:T(8,128)(2,1)S(1)}, bf16[112,1024]{1,0:T(8,128)(2,1)S(1)}, u32[]{:S(2)}, u32[]{:S(2)}) %collective-permute-start.25) | collective-permute-done | bytes 229408 | tf_op jit(solution)/shard_map/ppermute | solution.py:340
  23.0 1.0 %squeeze.8 = (bf16[352,1024]{1,0:T(8,128)(2,1)S(1)}, s32[1,512]{1,0:T(1,128)S(1)}) custom-call(bf16[112,1024]{1,0:T(8,128)(2,1)S(1)} %collective-permute-done.22.refs_0_, bf16[112,1024]{1,0:T(8,128)(2,1)S(1)} %collective-permute-done.23.refs_1_, bf16[112,1024]{1,0:T(8,128)(2,1)S(1)} %collective-permute-done.24.refs_2_, ...), custom_call_target="tpu_custom_call" | custom-call | flops 369098752 | bytes 1769472 | tf_op jit(solution)/shard_map/squeeze/pallas_call | solution.py:125
  24.1 0.7 collective-permute-start.26
  24.8 0.7 collective-permute-start.27
  25.5 6.1 %collective-permute-start.28 = (bf16[352,1024]{1,0:T(8,128)(2,1)S(1)}, bf16[352,1024]{1,0:T(8,128)(2,1)S(1)}, u32[]{:S(2)}, u32[]{:S(2)}) collective-permute-start(bf16[352,1024]{1,0:T(8,128)(2,1)S(1)} %get-tuple-element.74.refs_0_), channel_id=1, source_target_pairs={{0,2},{7,5},{8,10},{15,13},{16,18},{23,21},{24,26},{31,29}} | collective-permute-start | bytes 2162696 | tf_op jit(solution)/shard_map/ppermute | solution.py:354
  31.6 0.0 collective-permute-done.13.refs_0_
  31.6 0.7 collective-permute-start.14
  32.2 8.1 %collective-permute-done.14.refs_1_ = bf16[112,1024]{1,0:T(8,128)(2,1)S(1)} collective-permute-done((bf16[112,1024]{1,0:T(8,128)(2,1)S(1)}, bf16[112,1024]{1,0:T(8,128)(2,1)S(1)}, u32[]{:S(2)}, u32[]{:S(2)}) %collective-permute-start.14) | collective-permute-done | bytes 229408 | tf_op jit(solution)/shard_map/ppermute | solution.py:340
  40.3 1.4 %collective-permute-start.20 = (bf16[192,1024]{1,0:T(8,128)(2,1)}, bf16[192,1024]{1,0:T(8,128)(2,1)}, u32[]{:S(2)}, u32[]{:S(2)}) collective-permute-start(bf16[192,1024]{1,0:T(8,128)(2,1)} %get-tuple-element.68.refs_0_), channel_id=1, source_target_pairs={{3,2},{4,5},{11,10},{12,13},{19,18},{20,21},{27,26},{28,29}} | collective-permute-start | bytes 1179656 | tf_op jit(solution)/shard_map/ppermute | solution.py:354
  41.8 0.0 collective-permute-done.19.refs_1_
  41.8 0.0 copy-start
  41.8 0.8 copy-done
  42.5 2.0 %collective-permute-start.21 = (bf16[192,1024]{1,0:T(8,128)(2,1)}, bf16[192,1024]{1,0:T(8,128)(2,1)}, u32[]{:S(2)}, u32[]{:S(2)}) collective-permute-start(bf16[192,1024]{1,0:T(8,128)(2,1)} %get-tuple-element.68.refs_0_), channel_id=1, source_target_pairs={{0,2},{7,5},{8,10},{15,13},{16,18},{23,21},{24,26},{31,29}} | collective-permute-start | bytes 1179656 | tf_op jit(solution)/shard_map/ppermute | solution.py:354
  44.6 0.8 squeeze.6
  45.4 0.0 collective-permute-done.20.refs_2_
  45.5 0.7 collective-permute-start.15
  46.2 7.6 %collective-permute-done.21.refs_3_ = bf16[192,1024]{1,0:T(8,128)(2,1)} collective-permute-done((bf16[192,1024]{1,0:T(8,128)(2,1)}, bf16[192,1024]{1,0:T(8,128)(2,1)}, u32[]{:S(2)}, u32[]{:S(2)}) %collective-permute-start.21) | collective-permute-done | bytes 393248 | tf_op jit(solution)/shard_map/ppermute | solution.py:354
  53.7 0.7 collective-permute-start.16
  54.4 0.0 copy-start.1
  54.4 1.0 %copy-done.1 = bf16[192,1024]{1,0:T(8,128)(2,1)S(1)} copy-done((bf16[192,1024]{1,0:T(8,128)(2,1)S(1)}, bf16[192,1024]{1,0:T(8,128)(2,1)}, u32[]{:S(2)}) %copy-start.1) | copy-done | bytes 393240
  55.4 1.2 %pair.3 = (bf16[768,1024]{1,0:T(8,128)(2,1)S(1)}, f32[1,768]{1,0:T(1,128)S(1)}, f32[1,768]{1,0:T(1,128)S(1)}) custom-call(s32[1]{0:T(128)} %bitcast.5.owner_ref, bf16[192,1024]{1,0:T(8,128)(2,1)} %get-tuple-element.68.refs_0_, bf16[192,1024]{1,0:T(8,128)(2,1)S(1)} %copy-done.1, bf16[192,1024]{1,0:T(8,128)(2,1)} %collective-permute-done.20.refs_2_, ...), custom_call_target="tpu_custom_call" | custom-call | flops 603979776 | bytes 1572864 | tf_op jit(solution)/shard_map/pair/pallas_call | solution.py:208
  56.6 0.0 collective-permute-done.26.refs_1_
  56.6 8.8 %collective-permute-start.17 = (bf16[192,1024]{1,0:T(8,128)(2,1)S(1)}, bf16[192,1024]{1,0:T(8,128)(2,1)S(1)}, u32[]{:S(2)}, u32[]{:S(2)}) collective-permute-start(bf16[192,1024]{1,0:T(8,128)(2,1)S(1)} %get-tuple-element.65.refs_0_), channel_id=1, source_target_pairs={{0,2},{7,5},{8,10},{15,13},{16,18},{23,21},{24,26},{31,29}} | collective-permute-start | bytes 1179656 | tf_op jit(solution)/shard_map/ppermute | solution.py:354
  65.4 0.0 collective-permute-done.27.refs_2_
  65.4 0.7 collective-permute-start.29
  66.1 0.0 collective-permute-done.28.refs_3_
  66.1 0.7 collective-permute-start.30
  66.8 0.0 collective-permute-done.15.refs_1_
  66.8 8.8 %collective-permute-start.31 = (s32[1,1024]{1,0:T(1,128)S(1)}, s32[1,1024]{1,0:T(1,128)S(1)}, u32[]{:S(2)}, u32[]{:S(2)}) collective-permute-start(s32[1,1024]{1,0:T(1,128)S(1)} %constant_dynamic-update-slice_fusion.refs_3_), channel_id=1, source_target_pairs={{0,2},{7,5},{8,10},{15,13},{16,18},{23,21},{24,26},{31,29}} | collective-permute-start | bytes 12296 | tf_op jit(solution)/shard_map/ppermute | solution.py:364
  75.6 0.0 collective-permute-done.16.refs_2_
  75.6 0.0 collective-permute-done.17.refs_3_
  75.6 0.0 copy-start.2
  75.6 0.0 copy-start.3
  75.6 1.4 %pair.5 = (bf16[768,1024]{1,0:T(8,128)(2,1)}, f32[1,768]{1,0:T(1,128)}, f32[1,768]{1,0:T(1,128)S(1)}, f32[1,768]{1,0:T(1,128)S(1)}, f32[1,1408]{1,0:T(1,128)S(1)}) custom-call(s32[1]{0:T(128)} %bitcast.5.owner_ref, bf16[192,1024]{1,0:T(8,128)(2,1)S(1)} %get-tuple-element.65.refs_0_, bf16[192,1024]{1,0:T(8,128)(2,1)S(1)} %collective-permute-done.15.refs_1_, ...), custom_call_target="tpu_custom_call" | custom-call | flops 4026531840 | bytes 1572864 | tf_op jit(solution)/shard_map/pair/pallas_call | solution.py:208
  77.0 0.0 collective-permute-done.29.refs_4_
  77.0 0.0 collective-permute-done.30.refs_5_
  77.0 0.0 collective-permute-done.31.refs_6_
  77.0 0.6 spread.3
  77.6 8.2 %all-to-all-start.1 = ((f32[32,1,128]{2,1,0:T(1,128)}), f32[32,1,128]{2,1,0:T(1,128)S(1)}, u32[]{:S(2)}, u32[]{:S(2)}) async-start(f32[32,1,128]{2,1,0:T(1,128)} %spread.3), calls=%async_computation.1 | async-start | bytes 32768 | tf_op jit(solution)/shard_map/all_to_all | solution.py:367
  85.9 7.2 %all-to-all-done.1.got_ref = f32[32,1,128]{2,1,0:T(1,128)S(1)} async-done(((f32[32,1,128]{2,1,0:T(1,128)}), f32[32,1,128]{2,1,0:T(1,128)S(1)}, u32[]{:S(2)}, u32[]{:S(2)}) %all-to-all-start.1) | async-done | bytes 16416 | tf_op jit(solution)/shard_map/all_to_all | solution.py:367
  93.1 1.1 %pick.3 = (f32[1,512]{1,0:T(1,128)}, s32[1]{0:T(128)}) custom-call(s32[1,512]{1,0:T(1,128)S(1)} %get-tuple-element.62.pos_ref, f32[32,1,128]{2,1,0:T(1,128)S(1)} %all-to-all-done.1.got_ref), custom_call_target="tpu_custom_call" | custom-call | tf_op jit(solution)/shard_map/pick/pallas_call | solution.py:319
  94.8 0.0 copy-done.2
  94.8 0.0 copy-done.3
  (5 shorter events, 0.0 us)
Async XLA Ops:
  2.9 4.9 %collective-permute-start.18 = (bf16[112,1024]{1,0:T(8,128)(2,1)S(1)}, bf16[112,1024]{1,0:T(8,128)(2,1)S(1)}, u32[]{:S(2)}, u32[]{:S(2)}) collective-permute-start(bf16[112,1024]{1,0:T(8,128)(2,1)S(1)} %get-tuple-element.67), channel_id=1, source_target_pairs={{0,4},{4,0},{8,12},{12,8},{16,20},{20,16},{24,28},{28,24},{1,5},{5... | collective-permute-start | bytes 688136 | tf_op jit(solution)/shard_map/ppermute | solution.py:340
  3.5 9.0 %collective-permute-start.22 = (bf16[112,1024]{1,0:T(8,128)(2,1)S(1)}, bf16[112,1024]{1,0:T(8,128)(2,1)S(1)}, u32[]{:S(2)}, u32[]{:S(2)}) collective-permute-start(bf16[112,1024]{1,0:T(8,128)(2,1)S(1)} %get-tuple-element.70), channel_id=1, source_target_pairs={{0,8},{4,12},{8,0},{12,4},{16,24},{20,28},{24,16},{28,20},{1,9},{5... | collective-permute-start | bytes 688136 | tf_op jit(solution)/shard_map/ppermute | solution.py:340
  6.0 10.9 %collective-permute-start.23 = (bf16[112,1024]{1,0:T(8,128)(2,1)S(1)}, bf16[112,1024]{1,0:T(8,128)(2,1)S(1)}, u32[]{:S(2)}, u32[]{:S(2)}) collective-permute-start(bf16[112,1024]{1,0:T(8,128)(2,1)S(1)} %get-tuple-element.71), channel_id=1, source_target_pairs={{0,12},{4,8},{8,4},{12,0},{16,28},{20,24},{24,20},{28,16},{1,13},{... | collective-permute-start | bytes 688136 | tf_op jit(solution)/shard_map/ppermute | solution.py:340
  6.0 10.9 %collective-permute-start.24 = (bf16[112,1024]{1,0:T(8,128)(2,1)S(1)}, bf16[112,1024]{1,0:T(8,128)(2,1)S(1)}, u32[]{:S(2)}, u32[]{:S(2)}) collective-permute-start(bf16[112,1024]{1,0:T(8,128)(2,1)S(1)} %get-tuple-element.72), channel_id=1, source_target_pairs={{0,16},{4,20},{8,24},{12,28},{16,0},{20,4},{24,8},{28,12},{1,17},{... | collective-permute-start | bytes 688136 | tf_op jit(solution)/shard_map/ppermute | solution.py:340
  7.8 15.2 %collective-permute-start.25 = (bf16[112,1024]{1,0:T(8,128)(2,1)S(1)}, bf16[112,1024]{1,0:T(8,128)(2,1)S(1)}, u32[]{:S(2)}, u32[]{:S(2)}) collective-permute-start(bf16[112,1024]{1,0:T(8,128)(2,1)S(1)} %get-tuple-element.73), channel_id=1, source_target_pairs={{0,20},{4,16},{8,28},{12,24},{16,4},{20,0},{24,12},{28,8},{1,21},{... | collective-permute-start | bytes 688136 | tf_op jit(solution)/shard_map/ppermute | solution.py:340
  7.8 23.7 %collective-permute-start.13 = (bf16[112,1024]{1,0:T(8,128)(2,1)S(1)}, bf16[112,1024]{1,0:T(8,128)(2,1)S(1)}, u32[]{:S(2)}, u32[]{:S(2)}) collective-permute-start(bf16[112,1024]{1,0:T(8,128)(2,1)S(1)} %get-tuple-element.63), channel_id=1, source_target_pairs={{0,24},{4,28},{8,16},{12,20},{16,8},{20,12},{24,0},{28,4},{1,25},{... | collective-permute-start | bytes 688136 | tf_op jit(solution)/shard_map/ppermute | solution.py:340
  12.5 29.3 %collective-permute-start.19 = (bf16[192,1024]{1,0:T(8,128)(2,1)}, bf16[192,1024]{1,0:T(8,128)(2,1)S(1)}, u32[]{:S(2)}, u32[]{:S(2)}) collective-permute-start(bf16[192,1024]{1,0:T(8,128)(2,1)} %get-tuple-element.68.refs_0_), channel_id=1, source_target_pairs={{1,2},{6,5},{9,10},{14,13},{17,18},{22,21},{25,26},{30,29}} | collective-permute-start | bytes 1179656 | tf_op jit(solution)/shard_map/ppermute | solution.py:354
  24.1 32.6 %collective-permute-start.26 = (bf16[352,1024]{1,0:T(8,128)(2,1)S(1)}, bf16[352,1024]{1,0:T(8,128)(2,1)S(1)}, u32[]{:S(2)}, u32[]{:S(2)}) collective-permute-start(bf16[352,1024]{1,0:T(8,128)(2,1)S(1)} %get-tuple-element.74.refs_0_), channel_id=1, source_target_pairs={{1,2},{6,5},{9,10},{14,13},{17,18},{22,21},{25,26},{30,29}} | collective-permute-start | bytes 2162696 | tf_op jit(solution)/shard_map/ppermute | solution.py:354
  24.8 40.6 %collective-permute-start.27 = (bf16[352,1024]{1,0:T(8,128)(2,1)S(1)}, bf16[352,1024]{1,0:T(8,128)(2,1)S(1)}, u32[]{:S(2)}, u32[]{:S(2)}) collective-permute-start(bf16[352,1024]{1,0:T(8,128)(2,1)S(1)} %get-tuple-element.74.refs_0_), channel_id=1, source_target_pairs={{3,2},{4,5},{11,10},{12,13},{19,18},{20,21},{27,26},{28,29}} | collective-permute-start | bytes 2162696 | tf_op jit(solution)/shard_map/ppermute | solution.py:354
  25.5 40.6 %collective-permute-start.28 = (bf16[352,1024]{1,0:T(8,128)(2,1)S(1)}, bf16[352,1024]{1,0:T(8,128)(2,1)S(1)}, u32[]{:S(2)}, u32[]{:S(2)}) collective-permute-start(bf16[352,1024]{1,0:T(8,128)(2,1)S(1)} %get-tuple-element.74.refs_0_), channel_id=1, source_target_pairs={{0,2},{7,5},{8,10},{15,13},{16,18},{23,21},{24,26},{31,29}} | collective-permute-start | bytes 2162696 | tf_op jit(solution)/shard_map/ppermute | solution.py:354
  31.6 8.8 %collective-permute-start.14 = (bf16[112,1024]{1,0:T(8,128)(2,1)S(1)}, bf16[112,1024]{1,0:T(8,128)(2,1)S(1)}, u32[]{:S(2)}, u32[]{:S(2)}) collective-permute-start(bf16[112,1024]{1,0:T(8,128)(2,1)S(1)} %get-tuple-element.64), channel_id=1, source_target_pairs={{0,28},{4,24},{8,20},{12,16},{16,12},{20,8},{24,4},{28,0},{1,29},{... | collective-permute-start | bytes 688136 | tf_op jit(solution)/shard_map/ppermute | solution.py:340
  40.3 5.1 %collective-permute-start.20 = (bf16[192,1024]{1,0:T(8,128)(2,1)}, bf16[192,1024]{1,0:T(8,128)(2,1)}, u32[]{:S(2)}, u32[]{:S(2)}) collective-permute-start(bf16[192,1024]{1,0:T(8,128)(2,1)} %get-tuple-element.68.refs_0_), channel_id=1, source_target_pairs={{3,2},{4,5},{11,10},{12,13},{19,18},{20,21},{27,26},{28,29}} | collective-permute-start | bytes 1179656 | tf_op jit(solution)/shard_map/ppermute | solution.py:354
  41.8 0.8 copy-start
  42.5 11.2 %collective-permute-start.21 = (bf16[192,1024]{1,0:T(8,128)(2,1)}, bf16[192,1024]{1,0:T(8,128)(2,1)}, u32[]{:S(2)}, u32[]{:S(2)}) collective-permute-start(bf16[192,1024]{1,0:T(8,128)(2,1)} %get-tuple-element.68.refs_0_), channel_id=1, source_target_pairs={{0,2},{7,5},{8,10},{15,13},{16,18},{23,21},{24,26},{31,29}} | collective-permute-start | bytes 1179656 | tf_op jit(solution)/shard_map/ppermute | solution.py:354
  45.5 21.3 %collective-permute-start.15 = (bf16[192,1024]{1,0:T(8,128)(2,1)S(1)}, bf16[192,1024]{1,0:T(8,128)(2,1)S(1)}, u32[]{:S(2)}, u32[]{:S(2)}) collective-permute-start(bf16[192,1024]{1,0:T(8,128)(2,1)S(1)} %get-tuple-element.65.refs_0_), channel_id=1, source_target_pairs={{1,2},{6,5},{9,10},{14,13},{17,18},{22,21},{25,26},{30,29}} | collective-permute-start | bytes 1179656 | tf_op jit(solution)/shard_map/ppermute | solution.py:354
  53.7 21.9 %collective-permute-start.16 = (bf16[192,1024]{1,0:T(8,128)(2,1)S(1)}, bf16[192,1024]{1,0:T(8,128)(2,1)S(1)}, u32[]{:S(2)}, u32[]{:S(2)}) collective-permute-start(bf16[192,1024]{1,0:T(8,128)(2,1)S(1)} %get-tuple-element.65.refs_0_), channel_id=1, source_target_pairs={{3,2},{4,5},{11,10},{12,13},{19,18},{20,21},{27,26},{28,29}} | collective-permute-start | bytes 1179656 | tf_op jit(solution)/shard_map/ppermute | solution.py:354
  54.4 1.0 %copy-start.1 = (bf16[192,1024]{1,0:T(8,128)(2,1)S(1)}, bf16[192,1024]{1,0:T(8,128)(2,1)}, u32[]{:S(2)}) copy-start(bf16[192,1024]{1,0:T(8,128)(2,1)} %copy-done) | copy-start | bytes 1179652
  56.6 19.0 %collective-permute-start.17 = (bf16[192,1024]{1,0:T(8,128)(2,1)S(1)}, bf16[192,1024]{1,0:T(8,128)(2,1)S(1)}, u32[]{:S(2)}, u32[]{:S(2)}) collective-permute-start(bf16[192,1024]{1,0:T(8,128)(2,1)S(1)} %get-tuple-element.65.refs_0_), channel_id=1, source_target_pairs={{0,2},{7,5},{8,10},{15,13},{16,18},{23,21},{24,26},{31,29}} | collective-permute-start | bytes 1179656 | tf_op jit(solution)/shard_map/ppermute | solution.py:354
  65.4 11.6 %collective-permute-start.29 = (s32[1,1024]{1,0:T(1,128)S(1)}, s32[1,1024]{1,0:T(1,128)S(1)}, u32[]{:S(2)}, u32[]{:S(2)}) collective-permute-start(s32[1,1024]{1,0:T(1,128)S(1)} %constant_dynamic-update-slice_fusion.refs_3_), channel_id=1, source_target_pairs={{1,2},{6,5},{9,10},{14,13},{17,18},{22,21},{25,26},{30,29}} | collective-permute-start | bytes 12296 | tf_op jit(solution)/shard_map/ppermute | solution.py:364
  66.1 10.9 %collective-permute-start.30 = (s32[1,1024]{1,0:T(1,128)S(1)}, s32[1,1024]{1,0:T(1,128)S(1)}, u32[]{:S(2)}, u32[]{:S(2)}) collective-permute-start(s32[1,1024]{1,0:T(1,128)S(1)} %constant_dynamic-update-slice_fusion.refs_3_), channel_id=1, source_target_pairs={{3,2},{4,5},{11,10},{12,13},{19,18},{20,21},{27,26},{28,29}} | collective-permute-start | bytes 12296 | tf_op jit(solution)/shard_map/ppermute | solution.py:364
  66.8 10.2 %collective-permute-start.31 = (s32[1,1024]{1,0:T(1,128)S(1)}, s32[1,1024]{1,0:T(1,128)S(1)}, u32[]{:S(2)}, u32[]{:S(2)}) collective-permute-start(s32[1,1024]{1,0:T(1,128)S(1)} %constant_dynamic-update-slice_fusion.refs_3_), channel_id=1, source_target_pairs={{0,2},{7,5},{8,10},{15,13},{16,18},{23,21},{24,26},{31,29}} | collective-permute-start | bytes 12296 | tf_op jit(solution)/shard_map/ppermute | solution.py:364
  75.6 19.2 %copy-start.2 = (bf16[512,1024]{1,0:T(8,128)(2,1)S(1)}, bf16[512,1024]{1,0:T(8,128)(2,1)}, u32[]{:S(2)}) copy-start(bf16[512,1024]{1,0:T(8,128)(2,1)} %embed_hbm.1) | copy-start | bytes 3145732
  75.6 19.2 %copy-start.3 = (s32[512]{0:T(512)S(1)}, s32[512]{0:T(512)}, u32[]{:S(2)}) copy-start(s32[512]{0:T(512)} %param.6) | copy-start | bytes 6148
  77.6 15.4 %all-to-all-start.1 = ((f32[32,1,128]{2,1,0:T(1,128)}), f32[32,1,128]{2,1,0:T(1,128)S(1)}, u32[]{:S(2)}, u32[]{:S(2)}) async-start(f32[32,1,128]{2,1,0:T(1,128)} %spread.3), calls=%async_computation.1 | async-start | bytes 32768 | tf_op jit(solution)/shard_map/all_to_all | solution.py:367

commit v2 on v1

--- a/solution.py
+++ b/solution.py
@@ -21,8 +21,8 @@
 
 
 def pack_kernel(nsec, cap, stride, nblk, me_ref, dest_hbm, embed_hbm, *refs):
-    pos_ref, sections = refs[0], refs[1 : nsec + 1]
-    dest_ref, embed_ref, dest_sem, embed_sem = refs[nsec + 1 :]
+    pos_ref, place_ref, held_ref, unit_ref, *sections = refs[:-4]
+    dest_ref, embed_ref, dest_sem, embed_sem = refs[-4:]
     dest_copy = pltpu.make_async_copy(dest_hbm, dest_ref, dest_sem)
     embed_copy = pltpu.make_async_copy(embed_hbm, embed_ref, embed_sem)
     dest_copy.start()
@@ -41,39 +41,65 @@
     pos_ref[...] = jnp.where(rank < cap, cluster * stride + rank, -1)
     pos = jnp.where(rank < cap, part * cap + rank, -1)
     held = jnp.sum(onehot.astype(F32), axis=1, keepdims=True)
-    rows = lax.broadcasted_iota(jnp.int32, (cap, 128), 0).astype(F32)
-    first = lax.broadcasted_iota(jnp.int32, (cap, 128), 1) == 0
+    place_ref[...] = pos
+    held_ref[...] = held
     embed_copy.wait()
     wide = embed_ref[...].astype(F32)
     unit = (wide * lax.rsqrt(jnp.sum(wide * wide, axis=1, keepdims=True) + 1e-06)).astype(BF16)
+    unit_ref[...] = unit
+    fill(unit, pos, held, sections, 0, cap)
+
+
+def fill(unit, pos, held, sections, base, cap):
+    rows = lax.broadcasted_iota(jnp.int32, (cap, 128), 0).astype(F32)
+    first = lax.broadcasted_iota(jnp.int32, (cap, 128), 1) == 0
+    number = len(sections) * cap
+    pick = lax.broadcasted_iota(jnp.int32, (number, pos.shape[1]), 0) + base * cap == pos
+    packed = jnp.dot(pick.astype(F32).astype(BF16), unit, preferred_element_type=F32)
     for k, out in enumerate(sections):
-        pick = lax.broadcasted_iota(jnp.int32, (cap, count), 0) + k * cap == pos
-        value = jnp.dot(pick.astype(F32).astype(BF16), unit, preferred_element_type=F32)
+        value = packed[k * cap : (k + 1) * cap, :]
         out[...] = value.astype(BF16)
-        many = held[k : k + 1, :]
+        many = held[base + k : base + k + 1, :]
         head = jnp.where(first & (rows >= many), PAD, value[:, 0:128])
         head = jnp.where(first & (rows == cap - 1.0) & (many > cap), FULL, head)
         out[:, 0:128] = head.astype(BF16)
 
 
-def pack(embed, dest, me, nsec, cap, stride, nblk):
+def rest_kernel(base, cap, unit_ref, place_ref, held_ref, *sections):
+    fill(unit_ref[...], place_ref[...], held_ref[...], sections, base, cap)
+
+
+def pack(embed, dest, me, nsec, now, cap, stride, nblk):
     count, width = embed.shape
     hbm = pl.BlockSpec(memory_space=pltpu.HBM)
-    return pl.pallas_call(
+    section = jax.ShapeDtypeStruct((cap, width), BF16)
+    places = jax.ShapeDtypeStruct((1, count), jnp.int32)
+    pos, place, held, unit, *sections = pl.pallas_call(
         functools.partial(pack_kernel, nsec, cap, stride, nblk),
-        out_shape=[jax.ShapeDtypeStruct((1, count), jnp.int32)]
-        + [jax.ShapeDtypeStruct((cap, width), BF16)] * nsec,
+        out_shape=[places, places, jax.ShapeDtypeStruct((nsec, 1), F32)]
+        + [jax.ShapeDtypeStruct((count, width), BF16)]
+        + [section] * now,
         in_specs=[SMEM, hbm, hbm],
-        out_specs=[VMEM] * (nsec + 1),
+        out_specs=[VMEM] * (now + 4),
         scratch_shapes=[
             pltpu.VMEM((1, count), jnp.int32),
             pltpu.VMEM((count, width), BF16),
             pltpu.SemaphoreType.DMA,
             pltpu.SemaphoreType.DMA,
         ],
-        compiler_params=pltpu.CompilerParams(vmem_limit_bytes=24 << 20),
+        compiler_params=pltpu.CompilerParams(vmem_limit_bytes=12 << 20),
         name="pack",
     )(me, dest.reshape(1, count), embed)
+    if now < nsec:
+        sections += pl.pallas_call(
+            functools.partial(rest_kernel, now, cap),
+            out_shape=[section] * (nsec - now),
+            in_specs=[VMEM] * 3,
+            out_specs=[VMEM] * (nsec - now),
+            compiler_params=pltpu.CompilerParams(vmem_limit_bytes=8 << 20),
+            name="rest",
+        )(unit, place, held)
+    return pos, sections
 
 
 def scores(left, right):
@@ -143,12 +169,14 @@
     return jnp.where(entries > 3.0, REDO, jnp.where(entries > 1.5, LOW, 0.0))
 
 
-def pair_kernel(nblk, nold, unroll, owner_ref, *refs):
+def pair_kernel(nblk, nold, last, unroll, owner_ref, *refs):
     refs = list(refs)
     take = lambda n: [refs.pop(0) for _ in range(n)]
     blocks, olds, bias_olds, best_olds = take(nblk), take(nold), take(nold), take(nold)
-    (new_ref, bias_ref, best_ref), best_outs = take(3), take(nold)
-    (acc_ref,) = take(1)
+    if last:
+        (best_ref, *best_outs), (new_ref, bias_ref, acc_ref) = take(1 + nold), take(3)
+    else:
+        (best_ref, *best_outs), (new_ref, bias_ref), (acc_ref,) = take(1 + nold), take(2), take(1)
     rows, size = new_ref.shape[0], blocks[0].shape[0]
     tiles = lambda n: [(lo, min(TILE, n - lo)) for lo in range(0, n, TILE)]
 
@@ -200,25 +228,26 @@
     return -(-n // m) * m
 
 
-def pair(owner, blocks, olds, biases, bests, unroll):
+def pair(owner, blocks, olds, biases, bests, last, unroll):
     nblk, (size, width) = len(blocks), blocks[0].shape
     rows, nold = nblk * size, len(olds)
     row = jax.ShapeDtypeStruct((1, rows), F32)
     flops = 2 * width * rows * (rows // 2 + sum(o.shape[0] for o in olds))
+    kept = [] if last else [jax.ShapeDtypeStruct((rows, width), BF16), row]
+    scratch = [pltpu.VMEM((rows, width), BF16), pltpu.VMEM((1, rows), F32)] if last else []
     out = pl.pallas_call(
-        functools.partial(pair_kernel, nblk, nold, unroll),
-        out_shape=[jax.ShapeDtypeStruct((rows, width), BF16), row, row]
-        + [jax.ShapeDtypeStruct(b.shape, F32) for b in bests],
+        functools.partial(pair_kernel, nblk, nold, last, unroll),
+        out_shape=[row] + [jax.ShapeDtypeStruct(b.shape, F32) for b in bests] + kept,
         in_specs=[SMEM] + [VMEM] * (nblk + 3 * nold),
-        out_specs=[VMEM] * (3 + nold),
-        scratch_shapes=[pltpu.VMEM((rows, 128), F32)],
+        out_specs=[VMEM] * (1 + nold + len(kept)),
+        scratch_shapes=scratch + [pltpu.VMEM((rows, 128), F32)],
         compiler_params=pltpu.CompilerParams(vmem_limit_bytes=24 << 20),
         cost_estimate=pl.CostEstimate(
             flops=flops, bytes_accessed=rows * width * 2, transcendentals=0
         ),
         name="pair",
     )(owner, *blocks, *olds, *biases, *bests)
-    return out[0], out[1], list(out[3:]) + [out[2]]
+    return list(out[1 : 1 + nold]) + [out[0]], out[1 + nold :]
 
 
 def every_kernel(nblk, owner_ref, *refs):
@@ -334,7 +363,7 @@
 
 
 def best_of_all(embed, dest, owner, me, cap, stride, parts, rooms, nsec, nblk):
-    pos, *sent = pack(embed, dest, me, nsec, cap, stride, nblk)
+    pos, sent = pack(embed, dest, me, nsec, parts[-1][0] or nsec, cap, stride, nblk)
     held = [sent[0]]
     for k in range(1, nsec):
         held.append(lax.ppermute(sent[k], "grp", xor(nsec, k)))
@@ -355,9 +384,10 @@
         if len(parts) == 1:
             bests = [every(owner, blocks)]
         else:
-            new, bias, bests = pair(owner, blocks, arrays, biases, bests, 3)
-            arrays.append(new)
-            biases.append(bias)
+            last = q == len(parts) - 1
+            bests, kept = pair(owner, blocks, arrays, biases, bests, last, 3)
+            arrays.extend(kept[:1])
+            biases.extend(kept[1:])
     place = jnp.concatenate(places, axis=1)
     spots = [place]
     for route in routes:

time: 95.4 us -> 97 us (1.017)
  starting transfers between devices: 48.3 us -> 50.5 us
  Pallas kernels: 10.6 us -> 9.34 us
    all_to_all x1, starting transfers between devices: 8.24 us -> 10.3 us  [best_of_all(): lax.all_to_all(sorted_out, AXES, split_axis=0, concat_axis=0, tiled=True)]
    ppermute x9, starting transfers between devices: 21.7 us -> 23 us  [best_of_all(): blocks.append(lax.ppermute(group, AXES, route))]
    ppermute x3, starting transfers between devices: 10.1 us -> 8.97 us  [best_of_all(): spots.append(lax.ppermute(place, AXES, route))]
    ppermute x3, waiting for transfers between devices: 0.01 us -> 1.05 us  [best_of_all(): spots.append(lax.ppermute(place, AXES, route))]
    pallas_call x3 -> x4, Pallas kernels: 2.62 us -> 1.84 us  [the longest x3 1.44 us: pair(): pl.pallas_call(functools.partial(pair_kernel, nblk, nold, last, unroll),...]
  transfers between devices with their start and end apart: 20 -> 20, of which waited for: 6 -> 6; matrix products, arithmetic and copies ran while one was open for 0% -> 0% of each run, Pallas kernels for 6% -> 5%
where the time goes in v2:
time: 97 us; the launch traced here: 96.6 us
  starting transfers between devices  50.5 us (52%)
  waiting for transfers between devices  33.8 us (35%)
  Pallas kernels  9.34 us (10%)
  local copies, waits for them, and re-layouts  1.81 us (2%)
  between operations  1.08 us (1%)
    ppermute x9, starting transfers between devices, best_of_all(): blocks.append(lax.ppermute(group, AXES, route))  23 us
    ppermute x7, waiting for transfers between devices, best_of_all(): held.append(lax.ppermute(sent[k], 'grp', xor(nsec, k)))  17.9 us
    all_to_all x1, starting transfers between devices, best_of_all(): lax.all_to_all(sorted_out, AXES, split_axis=0, concat_axis=0, tiled=True)  10.3 us
    ppermute x3, starting transfers between devices, best_of_all(): spots.append(lax.ppermute(place, AXES, route))  8.97 us
    ppermute x7, starting transfers between devices, best_of_all(): held.append(lax.ppermute(sent[k], 'grp', xor(nsec, k)))  8.3 us
    ppermute x9, waiting for transfers between devices, best_of_all(): blocks.append(lax.ppermute(group, AXES, route))  7.6 us
    all_to_all x1, waiting for transfers between devices, best_of_all(): lax.all_to_all(sorted_out, AXES, split_axis=0, concat_axis=0, tiled=True)  7.2 us
    pallas_call x3, Pallas kernels, squeeze(): pl.pallas_call(functools.partial(squeeze_kernel, len(sections), stride),...  3.42 us
  transfers between devices with their start and end apart: 20, of which 6 were waited for; matrix products, arithmetic and copies ran while one was open for 0% of the time, Pallas kernels for 5%

profile of v2, /device:TPU:0, one launch (start us, length us, event | category | flops | bytes accessed | tf_op | source)
XLA Modules:
  0.0 96.6 jit_solution(12352074770316745706)
XLA Ops:
  0.0 2.4 %pack.3 = (s32[1,512]{1,0:T(1,128)S(1)}, s32[1,512]{1,0:T(1,128)S(1)}, f32[8,1]{1,0:T(8,128)S(1)}, bf16[512,1024]{1,0:T(8,128)(2,1)S(1)}, bf16[112,1024]{1,0:T(8...) custom-call(s32[1]{0:T(128)} %bitcast.3.me_ref, ...), custom_call_target="tpu_custom_call" | custom-call | tf_op jit(solution)/shard_map/pack/pallas_call | solution.py:77
  2.4 0.6 collective-permute-start.18
  3.0 2.6 %collective-permute-start.22 = (bf16[112,1024]{1,0:T(8,128)(2,1)S(1)}, bf16[112,1024]{1,0:T(8,128)(2,1)S(1)}, u32[]{:S(2)}, u32[]{:S(2)}) collective-permute-start(bf16[112,1024]{1,0:T(8,128)(2,1)S(1)} %get-tuple-element.76), channel_id=1, source_target_pairs={{0,8},{4,12},{8,0},{12,4},{16,24},{20,28},{24,16},{28,20},{1,9},{5... | collective-permute-start | bytes 688136 | tf_op jit(solution)/shard_map/ppermute | solution.py:369
  5.5 0.0 collective-permute-start.23
  5.6 1.8 %collective-permute-start.24 = (bf16[112,1024]{1,0:T(8,128)(2,1)S(1)}, bf16[112,1024]{1,0:T(8,128)(2,1)S(1)}, u32[]{:S(2)}, u32[]{:S(2)}) collective-permute-start(bf16[112,1024]{1,0:T(8,128)(2,1)S(1)} %get-tuple-element.78), channel_id=1, source_target_pairs={{0,16},{4,20},{8,24},{12,28},{16,0},{20,4},{24,8},{28,12},{1,17},{... | collective-permute-start | bytes 688136 | tf_op jit(solution)/shard_map/ppermute | solution.py:369
  7.3 0.0 collective-permute-start.25
  7.3 0.4 rest.1
  7.8 0.0 collective-permute-done.18.refs_1_
  7.8 2.7 %collective-permute-start.13 = (bf16[112,1024]{1,0:T(8,128)(2,1)S(1)}, bf16[112,1024]{1,0:T(8,128)(2,1)S(1)}, u32[]{:S(2)}, u32[]{:S(2)}) collective-permute-start(bf16[112,1024]{1,0:T(8,128)(2,1)S(1)} %get-tuple-element.69), channel_id=1, source_target_pairs={{0,24},{4,28},{8,16},{12,20},{16,8},{20,12},{24,0},{28,4},{1,25},{... | collective-permute-start | bytes 688136 | tf_op jit(solution)/shard_map/ppermute | solution.py:369
  10.5 1.6 %squeeze.7 = (bf16[192,1024]{1,0:T(8,128)(2,1)}, s32[1,256]{1,0:T(1,128)S(1)}) custom-call(bf16[112,1024]{1,0:T(8,128)(2,1)S(1)} %get-tuple-element.72.refs_0_, bf16[112,1024]{1,0:T(8,128)(2,1)S(1)} %collective-permute-done.18.refs_1_), custom_call_target="tpu_custom_call" | custom-call | flops 100663296 | bytes 917504 | tf_op jit(solution)/shard_map/squeeze/pallas_call | solution.py:151
  12.0 0.0 collective-permute-done.22.refs_0_
  12.0 0.7 collective-permute-start.19
  12.7 3.7 %collective-permute-done.23.refs_1_ = bf16[112,1024]{1,0:T(8,128)(2,1)S(1)} collective-permute-done((bf16[112,1024]{1,0:T(8,128)(2,1)S(1)}, bf16[112,1024]{1,0:T(8,128)(2,1)S(1)}, u32[]{:S(2)}, u32[]{:S(2)}) %collective-permute-start.23) | collective-permute-done | bytes 229408 | tf_op jit(solution)/shard_map/ppermute | solution.py:369
  16.4 0.0 collective-permute-done.24.refs_2_
  16.4 6.1 %collective-permute-done.25.refs_3_ = bf16[112,1024]{1,0:T(8,128)(2,1)S(1)} collective-permute-done((bf16[112,1024]{1,0:T(8,128)(2,1)S(1)}, bf16[112,1024]{1,0:T(8,128)(2,1)S(1)}, u32[]{:S(2)}, u32[]{:S(2)}) %collective-permute-start.25) | collective-permute-done | bytes 229408 | tf_op jit(solution)/shard_map/ppermute | solution.py:369
  22.6 1.0 %squeeze.8 = (bf16[352,1024]{1,0:T(8,128)(2,1)S(1)}, s32[1,512]{1,0:T(1,128)S(1)}) custom-call(bf16[112,1024]{1,0:T(8,128)(2,1)S(1)} %collective-permute-done.22.refs_0_, bf16[112,1024]{1,0:T(8,128)(2,1)S(1)} %collective-permute-done.23.refs_1_, bf16[112,1024]{1,0:T(8,128)(2,1)S(1)} %collective-permute-done.24.refs_2_, ...), custom_call_target="tpu_custom_call" | custom-call | flops 369098752 | bytes 1769472 | tf_op jit(solution)/shard_map/squeeze/pallas_call | solution.py:151
  23.6 0.7 collective-permute-start.26
  24.3 0.7 collective-permute-start.27
  25.0 6.1 %collective-permute-start.28 = (bf16[352,1024]{1,0:T(8,128)(2,1)S(1)}, bf16[352,1024]{1,0:T(8,128)(2,1)S(1)}, u32[]{:S(2)}, u32[]{:S(2)}) collective-permute-start(bf16[352,1024]{1,0:T(8,128)(2,1)S(1)} %get-tuple-element.80.refs_0_), channel_id=1, source_target_pairs={{0,2},{7,5},{8,10},{15,13},{16,18},{23,21},{24,26},{31,29}} | collective-permute-start | bytes 2162696 | tf_op jit(solution)/shard_map/ppermute | solution.py:383
  31.1 0.0 collective-permute-done.13.refs_0_
  31.1 0.7 collective-permute-start.14
  31.8 8.1 %collective-permute-done.14.refs_1_ = bf16[112,1024]{1,0:T(8,128)(2,1)S(1)} collective-permute-done((bf16[112,1024]{1,0:T(8,128)(2,1)S(1)}, bf16[112,1024]{1,0:T(8,128)(2,1)S(1)}, u32[]{:S(2)}, u32[]{:S(2)}) %collective-permute-start.14) | collective-permute-done | bytes 229408 | tf_op jit(solution)/shard_map/ppermute | solution.py:369
  39.9 1.4 %collective-permute-start.20 = (bf16[192,1024]{1,0:T(8,128)(2,1)}, bf16[192,1024]{1,0:T(8,128)(2,1)}, u32[]{:S(2)}, u32[]{:S(2)}) collective-permute-start(bf16[192,1024]{1,0:T(8,128)(2,1)} %get-tuple-element.74.refs_0_), channel_id=1, source_target_pairs={{3,2},{4,5},{11,10},{12,13},{19,18},{20,21},{27,26},{28,29}} | collective-permute-start | bytes 1179656 | tf_op jit(solution)/shard_map/ppermute | solution.py:383
  41.3 0.0 collective-permute-done.19.refs_1_
  41.3 0.0 copy-start
  41.3 0.8 copy-done
  42.1 2.0 %collective-permute-start.21 = (bf16[192,1024]{1,0:T(8,128)(2,1)}, bf16[192,1024]{1,0:T(8,128)(2,1)}, u32[]{:S(2)}, u32[]{:S(2)}) collective-permute-start(bf16[192,1024]{1,0:T(8,128)(2,1)} %get-tuple-element.74.refs_0_), channel_id=1, source_target_pairs={{0,2},{7,5},{8,10},{15,13},{16,18},{23,21},{24,26},{31,29}} | collective-permute-start | bytes 1179656 | tf_op jit(solution)/shard_map/ppermute | solution.py:383
  44.1 0.8 squeeze.6
  45.0 0.0 collective-permute-done.20.refs_2_
  45.0 0.7 collective-permute-start.29
  45.7 7.6 %collective-permute-done.21.refs_3_ = bf16[192,1024]{1,0:T(8,128)(2,1)} collective-permute-done((bf16[192,1024]{1,0:T(8,128)(2,1)}, bf16[192,1024]{1,0:T(8,128)(2,1)}, u32[]{:S(2)}, u32[]{:S(2)}) %collective-permute-start.21) | collective-permute-done | bytes 393248 | tf_op jit(solution)/shard_map/ppermute | solution.py:383
  53.2 0.6 collective-permute-start.30
  53.9 0.0 copy-start.1
  53.9 1.0 %copy-done.1 = bf16[192,1024]{1,0:T(8,128)(2,1)S(1)} copy-done((bf16[192,1024]{1,0:T(8,128)(2,1)S(1)}, bf16[192,1024]{1,0:T(8,128)(2,1)}, u32[]{:S(2)}) %copy-start.1) | copy-done | bytes 393240
  54.9 1.2 %pair.3 = (f32[1,768]{1,0:T(1,128)S(1)}, bf16[768,1024]{1,0:T(8,128)(2,1)S(1)}, f32[1,768]{1,0:T(1,128)S(1)}) custom-call(s32[1]{0:T(128)} %bitcast.5.owner_ref, bf16[192,1024]{1,0:T(8,128)(2,1)} %get-tuple-element.74.refs_0_, bf16[192,1024]{1,0:T(8,128)(2,1)S(1)} %copy-done.1, bf16[192,1024]{1,0:T(8,128)(2,1)} %collective-permute-done.20.refs_2_, ...), custom_call_target="tpu_custom_call" | custom-call | flops 603979776 | bytes 1572864 | tf_op jit(solution)/shard_map/pair/pallas_call | solution.py:238
  56.1 0.0 collective-permute-done.26.refs_1_
  56.1 0.7 collective-permute-start.15
  56.8 0.0 collective-permute-done.27.refs_2_
  56.8 0.7 collective-permute-start.16
  57.5 0.0 collective-permute-done.28.refs_3_
  57.5 10.0 %collective-permute-start.17 = (bf16[192,1024]{1,0:T(8,128)(2,1)S(1)}, bf16[192,1024]{1,0:T(8,128)(2,1)S(1)}, u32[]{:S(2)}, u32[]{:S(2)}) collective-permute-start(bf16[192,1024]{1,0:T(8,128)(2,1)S(1)} %get-tuple-element.71.refs_0_), channel_id=1, source_target_pairs={{0,2},{7,5},{8,10},{15,13},{16,18},{23,21},{24,26},{31,29}} | collective-permute-start | bytes 1179656 | tf_op jit(solution)/shard_map/ppermute | solution.py:383
  67.5 0.0 collective-permute-done.15.refs_1_
  67.6 7.7 %collective-permute-start.31 = (s32[1,1024]{1,0:T(1,128)S(1)}, s32[1,1024]{1,0:T(1,128)S(1)}, u32[]{:S(2)}, u32[]{:S(2)}) collective-permute-start(s32[1,1024]{1,0:T(1,128)S(1)} %constant_dynamic-update-slice_fusion.refs_3_), channel_id=1, source_target_pairs={{0,2},{7,5},{8,10},{15,13},{16,18},{23,21},{24,26},{31,29}} | collective-permute-start | bytes 12296 | tf_op jit(solution)/shard_map/ppermute | solution.py:394
  75.2 0.0 collective-permute-done.16.refs_2_
  75.2 0.0 collective-permute-done.17.refs_3_
  75.3 0.0 copy-start.2
  75.3 0.0 copy-start.3
  75.3 0.2 pair.5
  75.5 0.0 collective-permute-done.29.refs_4_
  75.5 0.0 collective-permute-done.30.refs_5_
  75.5 1.0 %collective-permute-done.31.refs_6_ = s32[1,1024]{1,0:T(1,128)S(1)} collective-permute-done((s32[1,1024]{1,0:T(1,128)S(1)}, s32[1,1024]{1,0:T(1,128)S(1)}, u32[]{:S(2)}, u32[]{:S(2)}) %collective-permute-start.31) | collective-permute-done | bytes 4128 | tf_op jit(solution)/shard_map/ppermute | solution.py:394
  76.5 0.6 spread.3
  77.1 10.3 %all-to-all-start.1 = ((f32[32,1,128]{2,1,0:T(1,128)}), f32[32,1,128]{2,1,0:T(1,128)S(1)}, u32[]{:S(2)}, u32[]{:S(2)}) async-start(f32[32,1,128]{2,1,0:T(1,128)} %spread.3), calls=%async_computation.1 | async-start | bytes 32768 | tf_op jit(solution)/shard_map/all_to_all | solution.py:397
  87.5 7.2 %all-to-all-done.1.got_ref = f32[32,1,128]{2,1,0:T(1,128)S(1)} async-done(((f32[32,1,128]{2,1,0:T(1,128)}), f32[32,1,128]{2,1,0:T(1,128)S(1)}, u32[]{:S(2)}, u32[]{:S(2)}) %all-to-all-start.1) | async-done | bytes 16416 | tf_op jit(solution)/shard_map/all_to_all | solution.py:397
  94.7 1.1 %pick.3 = (f32[1,512]{1,0:T(1,128)}, s32[1]{0:T(128)}) custom-call(s32[1,512]{1,0:T(1,128)S(1)} %get-tuple-element.65.pos_ref, f32[32,1,128]{2,1,0:T(1,128)S(1)} %all-to-all-done.1.got_ref), custom_call_target="tpu_custom_call" | custom-call | tf_op jit(solution)/shard_map/pick/pallas_call | solution.py:348
  96.4 0.0 copy-done.2
  96.4 0.0 copy-done.3
  (5 shorter events, 0.0 us)
Async XLA Ops:
  2.4 5.3 %collective-permute-start.18 = (bf16[112,1024]{1,0:T(8,128)(2,1)S(1)}, bf16[112,1024]{1,0:T(8,128)(2,1)S(1)}, u32[]{:S(2)}, u32[]{:S(2)}) collective-permute-start(bf16[112,1024]{1,0:T(8,128)(2,1)S(1)} %get-tuple-element.73), channel_id=1, source_target_pairs={{0,4},{4,0},{8,12},{12,8},{16,20},{20,16},{24,28},{28,24},{1,5},{5... | collective-permute-start | bytes 688136 | tf_op jit(solution)/shard_map/ppermute | solution.py:369
  3.0 9.1 %collective-permute-start.22 = (bf16[112,1024]{1,0:T(8,128)(2,1)S(1)}, bf16[112,1024]{1,0:T(8,128)(2,1)S(1)}, u32[]{:S(2)}, u32[]{:S(2)}) collective-permute-start(bf16[112,1024]{1,0:T(8,128)(2,1)S(1)} %get-tuple-element.76), channel_id=1, source_target_pairs={{0,8},{4,12},{8,0},{12,4},{16,24},{20,28},{24,16},{28,20},{1,9},{5... | collective-permute-start | bytes 688136 | tf_op jit(solution)/shard_map/ppermute | solution.py:369
  5.5 10.9 %collective-permute-start.23 = (bf16[112,1024]{1,0:T(8,128)(2,1)S(1)}, bf16[112,1024]{1,0:T(8,128)(2,1)S(1)}, u32[]{:S(2)}, u32[]{:S(2)}) collective-permute-start(bf16[112,1024]{1,0:T(8,128)(2,1)S(1)} %get-tuple-element.77), channel_id=1, source_target_pairs={{0,12},{4,8},{8,4},{12,0},{16,28},{20,24},{24,20},{28,16},{1,13},{... | collective-permute-start | bytes 688136 | tf_op jit(solution)/shard_map/ppermute | solution.py:369
  5.6 10.9 %collective-permute-start.24 = (bf16[112,1024]{1,0:T(8,128)(2,1)S(1)}, bf16[112,1024]{1,0:T(8,128)(2,1)S(1)}, u32[]{:S(2)}, u32[]{:S(2)}) collective-permute-start(bf16[112,1024]{1,0:T(8,128)(2,1)S(1)} %get-tuple-element.78), channel_id=1, source_target_pairs={{0,16},{4,20},{8,24},{12,28},{16,0},{20,4},{24,8},{28,12},{1,17},{... | collective-permute-start | bytes 688136 | tf_op jit(solution)/shard_map/ppermute | solution.py:369
  7.3 15.2 %collective-permute-start.25 = (bf16[112,1024]{1,0:T(8,128)(2,1)S(1)}, bf16[112,1024]{1,0:T(8,128)(2,1)S(1)}, u32[]{:S(2)}, u32[]{:S(2)}) collective-permute-start(bf16[112,1024]{1,0:T(8,128)(2,1)S(1)} %get-tuple-element.79), channel_id=1, source_target_pairs={{0,20},{4,16},{8,28},{12,24},{16,4},{20,0},{24,12},{28,8},{1,21},{... | collective-permute-start | bytes 688136 | tf_op jit(solution)/shard_map/ppermute | solution.py:369
  7.8 23.3 %collective-permute-start.13 = (bf16[112,1024]{1,0:T(8,128)(2,1)S(1)}, bf16[112,1024]{1,0:T(8,128)(2,1)S(1)}, u32[]{:S(2)}, u32[]{:S(2)}) collective-permute-start(bf16[112,1024]{1,0:T(8,128)(2,1)S(1)} %get-tuple-element.69), channel_id=1, source_target_pairs={{0,24},{4,28},{8,16},{12,20},{16,8},{20,12},{24,0},{28,4},{1,25},{... | collective-permute-start | bytes 688136 | tf_op jit(solution)/shard_map/ppermute | solution.py:369
  12.0 29.3 %collective-permute-start.19 = (bf16[192,1024]{1,0:T(8,128)(2,1)}, bf16[192,1024]{1,0:T(8,128)(2,1)S(1)}, u32[]{:S(2)}, u32[]{:S(2)}) collective-permute-start(bf16[192,1024]{1,0:T(8,128)(2,1)} %get-tuple-element.74.refs_0_), channel_id=1, source_target_pairs={{1,2},{6,5},{9,10},{14,13},{17,18},{22,21},{25,26},{30,29}} | collective-permute-start | bytes 1179656 | tf_op jit(solution)/shard_map/ppermute | solution.py:383
  23.6 32.5 %collective-permute-start.26 = (bf16[352,1024]{1,0:T(8,128)(2,1)S(1)}, bf16[352,1024]{1,0:T(8,128)(2,1)S(1)}, u32[]{:S(2)}, u32[]{:S(2)}) collective-permute-start(bf16[352,1024]{1,0:T(8,128)(2,1)S(1)} %get-tuple-element.80.refs_0_), channel_id=1, source_target_pairs={{1,2},{6,5},{9,10},{14,13},{17,18},{22,21},{25,26},{30,29}} | collective-permute-start | bytes 2162696 | tf_op jit(solution)/shard_map/ppermute | solution.py:383
  24.3 32.5 %collective-permute-start.27 = (bf16[352,1024]{1,0:T(8,128)(2,1)S(1)}, bf16[352,1024]{1,0:T(8,128)(2,1)S(1)}, u32[]{:S(2)}, u32[]{:S(2)}) collective-permute-start(bf16[352,1024]{1,0:T(8,128)(2,1)S(1)} %get-tuple-element.80.refs_0_), channel_id=1, source_target_pairs={{3,2},{4,5},{11,10},{12,13},{19,18},{20,21},{27,26},{28,29}} | collective-permute-start | bytes 2162696 | tf_op jit(solution)/shard_map/ppermute | solution.py:383
  25.0 32.5 %collective-permute-start.28 = (bf16[352,1024]{1,0:T(8,128)(2,1)S(1)}, bf16[352,1024]{1,0:T(8,128)(2,1)S(1)}, u32[]{:S(2)}, u32[]{:S(2)}) collective-permute-start(bf16[352,1024]{1,0:T(8,128)(2,1)S(1)} %get-tuple-element.80.refs_0_), channel_id=1, source_target_pairs={{0,2},{7,5},{8,10},{15,13},{16,18},{23,21},{24,26},{31,29}} | collective-permute-start | bytes 2162696 | tf_op jit(solution)/shard_map/ppermute | solution.py:383
  31.1 8.8 %collective-permute-start.14 = (bf16[112,1024]{1,0:T(8,128)(2,1)S(1)}, bf16[112,1024]{1,0:T(8,128)(2,1)S(1)}, u32[]{:S(2)}, u32[]{:S(2)}) collective-permute-start(bf16[112,1024]{1,0:T(8,128)(2,1)S(1)} %get-tuple-element.70), channel_id=1, source_target_pairs={{0,28},{4,24},{8,20},{12,16},{16,12},{20,8},{24,4},{28,0},{1,29},{... | collective-permute-start | bytes 688136 | tf_op jit(solution)/shard_map/ppermute | solution.py:369
  39.9 5.1 %collective-permute-start.20 = (bf16[192,1024]{1,0:T(8,128)(2,1)}, bf16[192,1024]{1,0:T(8,128)(2,1)}, u32[]{:S(2)}, u32[]{:S(2)}) collective-permute-start(bf16[192,1024]{1,0:T(8,128)(2,1)} %get-tuple-element.74.refs_0_), channel_id=1, source_target_pairs={{3,2},{4,5},{11,10},{12,13},{19,18},{20,21},{27,26},{28,29}} | collective-permute-start | bytes 1179656 | tf_op jit(solution)/shard_map/ppermute | solution.py:383
  41.3 0.8 copy-start
  42.1 11.2 %collective-permute-start.21 = (bf16[192,1024]{1,0:T(8,128)(2,1)}, bf16[192,1024]{1,0:T(8,128)(2,1)}, u32[]{:S(2)}, u32[]{:S(2)}) collective-permute-start(bf16[192,1024]{1,0:T(8,128)(2,1)} %get-tuple-element.74.refs_0_), channel_id=1, source_target_pairs={{0,2},{7,5},{8,10},{15,13},{16,18},{23,21},{24,26},{31,29}} | collective-permute-start | bytes 1179656 | tf_op jit(solution)/shard_map/ppermute | solution.py:383
  45.0 30.5 %collective-permute-start.29 = (s32[1,1024]{1,0:T(1,128)S(1)}, s32[1,1024]{1,0:T(1,128)S(1)}, u32[]{:S(2)}, u32[]{:S(2)}) collective-permute-start(s32[1,1024]{1,0:T(1,128)S(1)} %constant_dynamic-update-slice_fusion.refs_3_), channel_id=1, source_target_pairs={{1,2},{6,5},{9,10},{14,13},{17,18},{22,21},{25,26},{30,29}} | collective-permute-start | bytes 12296 | tf_op jit(solution)/shard_map/ppermute | solution.py:394
  53.2 22.2 %collective-permute-start.30 = (s32[1,1024]{1,0:T(1,128)S(1)}, s32[1,1024]{1,0:T(1,128)S(1)}, u32[]{:S(2)}, u32[]{:S(2)}) collective-permute-start(s32[1,1024]{1,0:T(1,128)S(1)} %constant_dynamic-update-slice_fusion.refs_3_), channel_id=1, source_target_pairs={{3,2},{4,5},{11,10},{12,13},{19,18},{20,21},{27,26},{28,29}} | collective-permute-start | bytes 12296 | tf_op jit(solution)/shard_map/ppermute | solution.py:394
  53.9 1.0 %copy-start.1 = (bf16[192,1024]{1,0:T(8,128)(2,1)S(1)}, bf16[192,1024]{1,0:T(8,128)(2,1)}, u32[]{:S(2)}) copy-start(bf16[192,1024]{1,0:T(8,128)(2,1)} %copy-done) | copy-start | bytes 1179652
  56.1 11.4 %collective-permute-start.15 = (bf16[192,1024]{1,0:T(8,128)(2,1)S(1)}, bf16[192,1024]{1,0:T(8,128)(2,1)S(1)}, u32[]{:S(2)}, u32[]{:S(2)}) collective-permute-start(bf16[192,1024]{1,0:T(8,128)(2,1)S(1)} %get-tuple-element.71.refs_0_), channel_id=1, source_target_pairs={{1,2},{6,5},{9,10},{14,13},{17,18},{22,21},{25,26},{30,29}} | collective-permute-start | bytes 1179656 | tf_op jit(solution)/shard_map/ppermute | solution.py:383
  56.8 18.4 %collective-permute-start.16 = (bf16[192,1024]{1,0:T(8,128)(2,1)S(1)}, bf16[192,1024]{1,0:T(8,128)(2,1)S(1)}, u32[]{:S(2)}, u32[]{:S(2)}) collective-permute-start(bf16[192,1024]{1,0:T(8,128)(2,1)S(1)} %get-tuple-element.71.refs_0_), channel_id=1, source_target_pairs={{3,2},{4,5},{11,10},{12,13},{19,18},{20,21},{27,26},{28,29}} | collective-permute-start | bytes 1179656 | tf_op jit(solution)/shard_map/ppermute | solution.py:383
  57.5 17.7 %collective-permute-start.17 = (bf16[192,1024]{1,0:T(8,128)(2,1)S(1)}, bf16[192,1024]{1,0:T(8,128)(2,1)S(1)}, u32[]{:S(2)}, u32[]{:S(2)}) collective-permute-start(bf16[192,1024]{1,0:T(8,128)(2,1)S(1)} %get-tuple-element.71.refs_0_), channel_id=1, source_target_pairs={{0,2},{7,5},{8,10},{15,13},{16,18},{23,21},{24,26},{31,29}} | collective-permute-start | bytes 1179656 | tf_op jit(solution)/shard_map/ppermute | solution.py:383
  67.6 9.0 %collective-permute-start.31 = (s32[1,1024]{1,0:T(1,128)S(1)}, s32[1,1024]{1,0:T(1,128)S(1)}, u32[]{:S(2)}, u32[]{:S(2)}) collective-permute-start(s32[1,1024]{1,0:T(1,128)S(1)} %constant_dynamic-update-slice_fusion.refs_3_), channel_id=1, source_target_pairs={{0,2},{7,5},{8,10},{15,13},{16,18},{23,21},{24,26},{31,29}} | collective-permute-start | bytes 12296 | tf_op jit(solution)/shard_map/ppermute | solution.py:394
  75.3 21.1 %copy-start.2 = (bf16[512,1024]{1,0:T(8,128)(2,1)S(1)}, bf16[512,1024]{1,0:T(8,128)(2,1)}, u32[]{:S(2)}) copy-start(bf16[512,1024]{1,0:T(8,128)(2,1)} %embed_hbm.1) | copy-start | bytes 3145732
  75.3 21.1 %copy-start.3 = (s32[512]{0:T(512)S(1)}, s32[512]{0:T(512)}, u32[]{:S(2)}) copy-start(s32[512]{0:T(512)} %param.6) | copy-start | bytes 6148
  77.1 17.5 %all-to-all-start.1 = ((f32[32,1,128]{2,1,0:T(1,128)}), f32[32,1,128]{2,1,0:T(1,128)S(1)}, u32[]{:S(2)}, u32[]{:S(2)}) async-start(f32[32,1,128]{2,1,0:T(1,128)} %spread.3), calls=%async_computation.1 | async-start | bytes 32768 | tf_op jit(solution)/shard_map/all_to_all | solution.py:397
